TPU v7x, 256 devices: a whole 4x4x8 slice. The times are simulated.
256 devices in a mesh: tm: 16 (over x_lo, z), heads: 4 (over y), rep: 4 (over x_hi, core).
Axes of the slice: x: 4 (x_hi: 2, x_lo: 2; x = x_hi * 2 + x_lo), y: 4, z: 8, core: 2. Of those that a mesh axis runs over, the one named last changes fastest.
Arguments:
- queries: bfloat16 [16384, 2560], P(('tm', 'rep'), 'heads'), may hold values from -100 to 100
- keys: bfloat16 [16384, 2560], P(('tm', 'rep'), 'heads'), may hold values from -4 to 4
- values: bfloat16 [16384, 2560], P(('tm', 'rep'), 'heads'), may hold values from -6 to 6
- block_lists: int32 [128, 16], P(('tm', 'rep')), may hold values from 0 to 127, as said below
- list_counts: int32 [128], P(('tm', 'rep')), may hold values from 2 to 16, as said below
- out_weight: bfloat16 [2560, 5120], P('heads', 'rep'), may hold values from -0.125 to 0.125
- gate: float32 [5120], P('rep'), may hold values from 0.5 to 2
Outputs:
- branch: bfloat16 [16384, 5120], P(('tm', 'heads'), 'rep')
Inputs may be any that keep to these rules, and one draw needn't show every extreme that they name: `block_lists`: entry 0 of block b's list is b itself; only the first list_counts[b] entries count, the rest are arbitrary block numbers. `list_counts`: every draw has a block whose count is 16.
All inputs are finite; a program needn't handle non-finite values.
Results may differ from a plain program's by a relative error of at most 0.0085.
Values may be sent and summed in bfloat16 or wider, within the bound.
No kernel may reach another device: no remote copies, remote signals or barrier semaphores. Data moves between devices by JAX's collectives and lax.ppermute only.
A program may use at most 64 MiB of HBM per device.

v0:
```python
import functools
import math

import jax
import jax.numpy as jnp
from jax import lax
from jax.experimental import pallas as pl
from jax.experimental.pallas import tpu as pltpu
from jax.sharding import Mesh, PartitionSpec as P


HD = 128
BLOCK = 128
LIST = 16
HEADS = 5
ROWS = 2 * BLOCK
WIDTH = HEADS * HD
TAIL = 32
EMPTY = -1e30
SCALE2 = math.log2(math.e) / HD**0.5

SOURCES = [(0, 0), (0, 1)] + [(s * d, c) for d in (1, 2, 3) for s in (-1, 1) for c in (0, 1)] + [(4, 0), (4, 1)]


def shift(value, axes, size, steps):
    return lax.ppermute(value, axes, [(i, (i + steps) % size) for i in range(size)])


def shift_x(value, steps):
    at = [2 * (x % 2) + x // 2 for x in range(4)]
    return lax.ppermute(value, ("xlo", "xhi"), [(at[x], at[(x + steps) % 4]) for x in range(4)])


def swap_core(value):
    return lax.ppermute(value, "core", [(0, 1), (1, 0)])


def prepare_kernel(keys, values, out):
    for b in range(2):
        rows = slice(b * BLOCK, (b + 1) * BLOCK)
        for h in range(HEADS):
            cols = slice(h * HD, (h + 1) * HD)
            out[0, b * HEADS + h] = keys[rows, cols]
            out[1, b * HEADS + h] = values[rows, cols].T


def prepare(keys, values):
    return pl.pallas_call(
        prepare_kernel,
        out_shape=jax.ShapeDtypeStruct((2, 2 * HEADS, BLOCK, HD), jnp.bfloat16),
        name="prepare",
    )(keys, values)


def attention(first_pair, pairs, split, start, last, mask_ref, *refs):
    refs = list(refs)
    if not start:
        acc_in, ml_in = refs[:2]
        refs = refs[2:]
    sent, refs = refs[:4], refs[4:]
    count = pairs * 2 if split else pairs
    sources, refs = refs[:count], refs[count:]
    if last:
        outs, refs = refs[:4], refs[4:]
        acc_ref, part, out_sems, refs = refs[0], refs[1], refs[2], refs[3:]
    else:
        acc_ref, ml_ref, refs = refs[0].at[0], refs[1].at[0], refs[2:]
    q, kv, sems, scores, chosen = refs
    qb = pl.program_id(0)

    @pl.when(qb == 0)
    def _():
        copies = []
        for i, source in enumerate(sources):
            target = kv.at[i // 2, i % 2] if split else kv.at[i]
            copies.append(pltpu.make_async_copy(source, target, sems.at[i]))
        for i, source in enumerate(sent):
            copies.append(pltpu.make_async_copy(source, q.at[i], sems.at[count + i]))
        for copy in copies:
            copy.start()
        for copy in copies:
            copy.wait()

    n = jnp.int32(0)
    for b in range(2 * pairs):
        chosen[n] = jnp.int32(b)
        n = n + mask_ref[qb, 2 * first_pair + b]

    q_rows = pl.ds(pl.multiple_of((qb & 1) * BLOCK, BLOCK), BLOCK)

    def first_pass(i, tops):
        b = chosen[i]
        pair, tile = b >> 1, (b & 1) * HEADS
        new = []
        for h in range(HEADS):
            s = (
                lax.dot_general(
                    kv[pair, 0, tile + h],
                    q[qb >> 1, q_rows, h * HD : (h + 1) * HD],
                    (((1,), (1,)), ((), ())),
                    preferred_element_type=jnp.float32,
                )
                * SCALE2
            )
            scores[i, h] = s
            new.append(jnp.maximum(tops[h], jnp.max(s.reshape(16, 8, BLOCK), axis=0)))
        return tuple(new)

    tops = lax.fori_loop(0, n, first_pass, (jnp.full((8, BLOCK), EMPTY, jnp.float32),) * HEADS)

    peaks, olds = [], []
    for h in range(HEADS):
        rows = slice(h * HD, (h + 1) * HD)
        peak = jnp.max(tops[h], axis=0, keepdims=True)
        if start:
            acc_ref[rows, :] = jnp.zeros((HD, BLOCK), jnp.float32)
            olds.append(None)
        else:
            old = ml_in[0, h : h + 1, :]
            peak = jnp.maximum(peak, old)
            factor = jnp.exp2(old - peak)
            acc_ref[rows, :] = acc_in[0, rows, :] * factor
            olds.append(ml_in[0, 8 + h : 9 + h, :] * factor)
        peaks.append(peak)

    def second_pass(i, totals):
        b = chosen[i]
        pair, tile = b >> 1, (b & 1) * HEADS
        new = []
        for h in range(HEADS):
            rows = slice(h * HD, (h + 1) * HD)
            p = jnp.exp2(scores[i, h] - peaks[h])
            new.append(totals[h] + jnp.sum(p.reshape(16, 8, BLOCK), axis=0))
            acc_ref[rows, :] = acc_ref[rows, :] + jnp.dot(
                kv[pair, 1, tile + h], p.astype(jnp.bfloat16), preferred_element_type=jnp.float32
            )
        return tuple(new)

    totals = lax.fori_loop(0, n, second_pass, (jnp.zeros((8, BLOCK), jnp.float32),) * HEADS)

    line = lax.broadcasted_iota(jnp.int32, (8, BLOCK), 0)
    zero = jnp.zeros((8, BLOCK), jnp.float32)
    weights = []
    for h in range(HEADS):
        weight = jnp.sum(totals[h], axis=0, keepdims=True)
        weights.append(weight if olds[h] is None else weight + olds[h])
    if not last:
        tops_table, sums_table = zero, zero
        for h in range(HEADS):
            tops_table = jnp.where(line == h, peaks[h], tops_table)
            sums_table = jnp.where(line == h, weights[h], sums_table)
        ml_ref[0:8, :] = tops_table
        ml_ref[8:16, :] = sums_table
        return

    tables = [zero, zero, zero, zero]
    for h in range(HEADS):
        rows = slice(h * HD, (h + 1) * HD)
        some = weights[h] > 0.0
        weight = jnp.where(some, weights[h], 1.0)
        part[qb, rows, :] = (acc_ref[rows, :] * (1.0 / weight)).astype(jnp.bfloat16)
        lse = jnp.where(some, peaks[h] + jnp.log2(weight), EMPTY)
        for j in range(3):
            piece = lse.astype(jnp.bfloat16).astype(jnp.float32)
            tables[j] = jnp.where(line == h, piece, tables[j])
            lse = lse - piece
    part[qb, WIDTH : WIDTH + TAIL, :] = jnp.concatenate(tables, axis=0).astype(jnp.bfloat16)

    copies = [pltpu.make_async_copy(part.at[pl.ds(2 * r, 2)], outs[r], out_sems.at[r]) for r in range(4)]
    for r in range(4):
        pl.when(qb == 2 * r + 1)(copies[r].start)

    @pl.when(qb == 7)
    def _():
        for copy in copies:
            copy.wait()


def attend(mask, queries, state, sources, first_pair, pairs, last):
    start = state is None
    split = len(sources) == 2 * pairs
    one = lambda i, m: (i, 0, 0)
    state_specs = [pl.BlockSpec((1, WIDTH, BLOCK), one), pl.BlockSpec((1, 16, BLOCK), one)]
    state_shapes = [
        jax.ShapeDtypeStruct((8, WIDTH, BLOCK), jnp.float32),
        jax.ShapeDtypeStruct((8, 16, BLOCK), jnp.float32),
    ]
    scratch = [
        pltpu.VMEM((4, ROWS, WIDTH), jnp.bfloat16),
        pltpu.VMEM((pairs, 2, 2 * HEADS, BLOCK, HD), jnp.bfloat16),
        pltpu.SemaphoreType.DMA((len(sources) + 4,)),
        pltpu.VMEM((2 * pairs, HEADS, BLOCK, BLOCK), jnp.float32),
        pltpu.SMEM((2 * pairs,), jnp.int32),
    ]
    anywhere = pl.BlockSpec(memory_space=pl.ANY)
    if last:
        out_specs = [anywhere] * 4
        out_shape = [jax.ShapeDtypeStruct((2, WIDTH + TAIL, BLOCK), jnp.bfloat16)] * 4
        scratch = [
            pltpu.VMEM((WIDTH, BLOCK), jnp.float32),
            pltpu.VMEM((8, WIDTH + TAIL, BLOCK), jnp.bfloat16),
            pltpu.SemaphoreType.DMA((4,)),
        ] + scratch
    else:
        out_specs, out_shape = state_specs, state_shapes
    return pl.pallas_call(
        functools.partial(attention, first_pair, pairs, split, start, last),
        grid_spec=pltpu.PrefetchScalarGridSpec(
            num_scalar_prefetch=1,
            grid=(8,),
            in_specs=([] if start else state_specs) + [anywhere] * (4 + len(sources)),
            out_specs=out_specs,
            scratch_shapes=scratch,
        ),
        out_shape=out_shape,
        cost_estimate=pl.CostEstimate(
            flops=4 * 10**9, transcendentals=pairs * 4 * 5 * BLOCK**2, bytes_accessed=pairs * 2**20
        ),
    )(mask, *(state or ()), *queries, *sources)


def combine_kernel(own, one, two, three, out):
    parts = (own, one, two, three)
    for b in range(2):
        lses = []
        for part in parts:
            table = part[b, WIDTH : WIDTH + TAIL, :].astype(jnp.float32)
            lses.append(table[0:8] + table[8:16] + table[16:24])
        peak = functools.reduce(jnp.maximum, lses)
        shares = [jnp.exp2(lse - peak) for lse in lses]
        whole = 1.0 / (shares[0] + shares[1] + shares[2] + shares[3])
        shares = [share * whole for share in shares]
        for h in range(HEADS):
            rows = slice(h * HD, (h + 1) * HD)
            value = parts[0][b, rows, :].astype(jnp.float32) * shares[0][h : h + 1]
            for part, share in zip(parts[1:], shares[1:]):
                value = value + part[b, rows, :].astype(jnp.float32) * share[h : h + 1]
            out[b * BLOCK : (b + 1) * BLOCK, rows] = value.T.astype(jnp.bfloat16)


def combine(parts):
    return pl.pallas_call(
        combine_kernel,
        out_shape=jax.ShapeDtypeStruct((ROWS, WIDTH), jnp.bfloat16),
        name="combine",
    )(*parts)


def project_kernel(place_ref, a, b, c, d, w0, t1, b1, t2, b2, t3, b3, gate, out, rows):
    for j, piece in enumerate((a, b, c, d)):
        rows[place_ref[j]] = piece[...]
    dot = functools.partial(jnp.dot, preferred_element_type=jnp.float32)
    for i in range(out.shape[1] // 256):
        cols = slice(i * 256, (i + 1) * 256)
        value = dot(rows[0], w0[:, cols])
        for j, (top, bottom) in enumerate(((t1, b1), (t2, b2), (t3, b3))):
            value = value + dot(rows[j + 1, :, :CUT], top[:, cols])
            value = value + dot(rows[j + 1, :, CUT:], bottom[:, cols])
        out[:, cols] = (gate[:, cols] * value).astype(jnp.bfloat16)


def project(place, pieces, weights, gate):
    cols = weights[0].shape[1]
    vmem = pl.BlockSpec(memory_space=pltpu.VMEM)
    return pl.pallas_call(
        project_kernel,
        in_specs=[pl.BlockSpec(memory_space=pltpu.SMEM)] + [vmem] * (4 + len(weights) + 1),
        out_specs=vmem,
        scratch_shapes=[pltpu.VMEM((4, ROWS, WIDTH), jnp.bfloat16)],
        out_shape=jax.ShapeDtypeStruct((ROWS, cols), jnp.bfloat16),
        name="project",
    )(place, *pieces, *weights, gate[None, :])


CUT = 384


def stages(queries, keys, values, block_lists, list_counts, out_weight, gate):
    xlo, z, y = lax.axis_index("xlo"), lax.axis_index("z"), lax.axis_index("y")
    xhi, core = lax.axis_index("xhi"), lax.axis_index("core")

    own = prepare(keys, values)
    before, after, near = [own], [own], [own]
    near.append(swap_core(own))
    for d in (1, 2, 3):
        before.append(shift(before[-1], "z", 8, 1))
        after.append(shift(after[-1], "z", 8, -1))
        near += [before[d], swap_core(before[d])]
        near += [after[d], swap_core(after[d])]
    far_keys = shift(before[3][0], "z", 8, 1)
    far_values = shift(after[3][1], "z", 8, -1)
    far = [far_keys, far_values, swap_core(far_keys)]
    far.append(swap_core(far_values))

    top, bottom = out_weight[:CUT], out_weight[CUT:]
    t1 = shift(top, "y", 4, 1)
    b3 = shift(bottom, "y", 4, -1)
    b1 = shift(bottom, "y", 4, 1)
    t3 = shift(top, "y", 4, -1)
    t2 = shift(t1, "y", 4, 1)
    b2 = shift(b3, "y", 4, -1)
    weights = [out_weight, t1, b1, t2, b2, t3, b3]

    table = jnp.concatenate([block_lists, list_counts[:, None]], axis=1)
    tables, all_queries = [table], [queries]
    for r in (1, 2, 3):
        tables.append(shift_x(table, r))
        all_queries.append(shift_x(queries, r))
    tables = jnp.stack(tables).reshape(8, LIST + 1)

    steps = jnp.array([s for s, _ in SOURCES], jnp.int32)
    other = jnp.array([c for _, c in SOURCES], jnp.int32)
    quarter = 2 * xhi + jnp.bitwise_xor(other, core)
    first = ((xlo * 8 + (z + steps) % 8) * 4 + quarter) * 2
    ids = (first[:, None] + jnp.arange(2)[None, :]).reshape(-1)
    used = jnp.arange(LIST)[None, :] < tables[:, LIST:]
    mask = jnp.any((tables[:, :LIST, None] == ids[None, None, :]) & used[:, :, None], axis=1).astype(jnp.int32)

    state = attend(mask, all_queries, None, near[:6], 0, 6, False)
    state = attend(mask, all_queries, state, near[6:10], 6, 4, False)
    state = attend(mask, all_queries, state, near[10:], 10, 4, False)
    parts = attend(mask, all_queries, state, far, 14, 2, True)

    back = [parts[0]]
    for r in (1, 2, 3):
        back.append(shift_x(parts[r], -r))
    attended = combine(back)

    places = [(i, j) for i in range(4) for j in range(4)]
    here = lax.ppermute(attended, ("y", "xhi", "core"), [(4 * i + j, 4 * j + i) for i, j in places])
    there = lax.ppermute(attended, ("y", "xhi", "core"), [(4 * i + j, 4 * j + (i ^ 2)) for i, j in places])
    pieces = [here, there, swap_core(here)]
    pieces.append(swap_core(there))
    groups = jnp.stack([2 * xhi + core, 2 * (1 - xhi) + core, 2 * xhi + 1 - core, 2 * (1 - xhi) + 1 - core])
    place = ((y - groups) % 4).astype(jnp.int32)
    return project(place, pieces, weights, gate)


def solution(mesh):
    fine = Mesh(mesh.devices.reshape(2, 8, 4, 2, 2), ("xlo", "z", "y", "xhi", "core"))
    rows, rep = ("xlo", "z", "xhi", "core"), ("xhi", "core")
    placed = (P(rows, "y"), P(rows, "y"), P(rows, "y"), P(rows, None), P(rows), P("y", rep), P(rep))
    return jax.shard_map(stages, mesh=fine, in_specs=placed, out_specs=P(("xlo", "z", "y"), rep), check_vma=False)
```

profile of v0, /device:TPU:1, one launch (start us, length us, event | category | flops | bytes accessed | tf_op | source)
XLA Modules:
  0.0 158.8 jit_solution(10281794393092229546)
XLA Ops:
  0.0 2.1 %prepare.1.refs_4_ = bf16[2,10,128,128]{3,2,1,0:T(8,128)(2,1)} custom-call(bf16[256,640]{1,0:T(8,128)(2,1)} %keys.1, bf16[256,640]{1,0:T(8,128)(2,1)} %values.1), custom_call_target="tpu_custom_call" | custom-call | tf_op jit(solution)/shard_map/prepare/pallas_call | solution.py:48
  2.1 2.5 %collective-permute-start.7 = (bf16[2,10,128,128]{3,2,1,0:T(8,128)(2,1)}, bf16[2,10,128,128]{3,2,1,0:T(8,128)(2,1)S(1)}, u32[]{:S(2)}, u32[]{:S(2)}) collective-permute-start(bf16[2,10,128,128]{3,2,1,0:T(8,128)(2,1)} %prepare.1.refs_4_), channel_id=1, source_target_pairs={{0,16},{16,32},{32,48},{48,64},{64,80},{80,96},{96,112},{112,0},{1... | collective-permute-start | bytes 1966088 | tf_op jit(solution)/shard_map/ppermute | solution.py:26
  4.5 3.9 %collective-permute-start.9 = (bf16[2,10,128,128]{3,2,1,0:T(8,128)(2,1)}, bf16[2,10,128,128]{3,2,1,0:T(8,128)(2,1)S(1)}, u32[]{:S(2)}, u32[]{:S(2)}) collective-permute-start(bf16[2,10,128,128]{3,2,1,0:T(8,128)(2,1)} %prepare.1.refs_4_), channel_id=1, source_target_pairs={{0,112},{16,0},{32,16},{48,32},{64,48},{80,64},{96,80},{112,96},{1... | collective-permute-start | bytes 1966088 | tf_op jit(solution)/shard_map/ppermute | solution.py:26
  10.0 2.5 %collective-permute-start.2 = (s32[2,17]{1,0:T(2,128)S(1)}, s32[2,17]{1,0:T(2,128)S(1)}, u32[]{:S(2)}, u32[]{:S(2)}) collective-permute-start(s32[2,17]{1,0:T(2,128)S(1)} %pad_add_fusion.1), channel_id=1, source_target_pairs={{0,130},{128,0},{2,128},{130,2},{1,131},{129,1},{3,129},{131,3},{4... | collective-permute-start | bytes 416 | tf_op jit(solution)/shard_map/ppermute | solution.py:31
  13.6 1.5 collective-permute-start.3
  18.1 5.1 %collective-permute-done.7.refs_6_ = bf16[2,10,128,128]{3,2,1,0:T(8,128)(2,1)S(1)} collective-permute-done((bf16[2,10,128,128]{3,2,1,0:T(8,128)(2,1)}, bf16[2,10,128,128]{3,2,1,0:T(8,128)(2,1)S(1)}, u32[]{:S(2)}, u32[]{:S(2)}) %collective-permute-start.7) | collective-permute-done | bytes 655392 | tf_op jit(solution)/shard_map/ppermute | solution.py:26
  23.1 2.7 %collective-permute-start.13 = (bf16[2,10,128,128]{3,2,1,0:T(8,128)(2,1)S(1)}, bf16[2,10,128,128]{3,2,1,0:T(8,128)(2,1)}, u32[]{:S(2)}, u32[]{:S(2)}) collective-permute-start(bf16[2,10,128,128]{3,2,1,0:T(8,128)(2,1)S(1)} %collective-permute-done.9.refs_8_), channel_id=1, source_target_pairs={{0,112},{16,0},{32,16},{48,32},{64,48},{80,64},{96,80},{112,96},{1... | collective-permute-start | bytes 1966088 | tf_op jit(solution)/shard_map/ppermute | solution.py:26
  26.5 1.9 %collective-permute-start.6 = (bf16[2,10,128,128]{3,2,1,0:T(8,128)(2,1)}, bf16[2,10,128,128]{3,2,1,0:T(8,128)(2,1)}, u32[]{:S(2)}, u32[]{:S(2)}) collective-permute-start(bf16[2,10,128,128]{3,2,1,0:T(8,128)(2,1)} %prepare.1.refs_4_), channel_id=1, source_target_pairs={{0,1},{1,0},{2,3},{3,2},{4,5},{5,4},{6,7},{7,6},{8,9},{9,8},{10,11... | collective-permute-start | bytes 1966088 | tf_op jit(solution)/shard_map/ppermute | solution.py:35
  28.4 2.4 %collective-permute-done.4.refs_2_.refs_4_ = bf16[256,640]{1,0:T(8,128)(2,1)S(1)} collective-permute-done((bf16[256,640]{1,0:T(8,128)(2,1)}, bf16[256,640]{1,0:T(8,128)(2,1)S(1)}, u32[]{:S(2)}, u32[]{:S(2)}) %collective-permute-start.4) | collective-permute-done | bytes 327712 | tf_op jit(solution)/shard_map/ppermute | solution.py:31
  30.8 2.7 %collective-permute-start.8 = (bf16[2,10,128,128]{3,2,1,0:T(8,128)(2,1)S(1)}, bf16[2,10,128,128]{3,2,1,0:T(8,128)(2,1)}, u32[]{:S(2)}, u32[]{:S(2)}) collective-permute-start(bf16[2,10,128,128]{3,2,1,0:T(8,128)(2,1)S(1)} %collective-permute-done.7.refs_6_), channel_id=1, source_target_pairs={{0,1},{1,0},{2,3},{3,2},{4,5},{5,4},{6,7},{7,6},{8,9},{9,8},{10,11... | collective-permute-start | bytes 1966088 | tf_op jit(solution)/shard_map/ppermute | solution.py:35
  35.5 2.0 %slice.26 = bf16[256,1280]{1,0:T(8,128)(2,1)} slice(bf16[640,1280]{1,0:T(8,128)(2,1)} %w0.1), slice={[384:640], [0:1280]} | slice | bytes 1310720 | tf_op jit(solution)/shard_map/slice | solution.py:295
  37.9 1.6 %collective-permute-done.11.refs_6_ = bf16[2,10,128,128]{3,2,1,0:T(8,128)(2,1)} collective-permute-done((bf16[2,10,128,128]{3,2,1,0:T(8,128)(2,1)S(1)}, bf16[2,10,128,128]{3,2,1,0:T(8,128)(2,1)}, u32[]{:S(2)}, u32[]{:S(2)}) %collective-permute-start.11) | collective-permute-done | bytes 655392 | tf_op jit(solution)/shard_map/ppermute | solution.py:26
  39.5 2.7 %collective-permute-start.17 = (bf16[2,10,128,128]{3,2,1,0:T(8,128)(2,1)}, bf16[2,10,128,128]{3,2,1,0:T(8,128)(2,1)}, u32[]{:S(2)}, u32[]{:S(2)}) collective-permute-start(bf16[2,10,128,128]{3,2,1,0:T(8,128)(2,1)} %collective-permute-done.13.refs_8_), channel_id=1, source_target_pairs={{0,112},{16,0},{32,16},{48,32},{64,48},{80,64},{96,80},{112,96},{1... | collective-permute-start | bytes 1966088 | tf_op jit(solution)/shard_map/ppermute | solution.py:26
  42.9 1.3 collective-permute-start.30
  44.2 2.9 %collective-permute-start.12 = (bf16[2,10,128,128]{3,2,1,0:T(8,128)(2,1)}, bf16[2,10,128,128]{3,2,1,0:T(8,128)(2,1)}, u32[]{:S(2)}, u32[]{:S(2)}) collective-permute-start(bf16[2,10,128,128]{3,2,1,0:T(8,128)(2,1)} %collective-permute-done.11.refs_6_), channel_id=1, source_target_pairs={{0,1},{1,0},{2,3},{3,2},{4,5},{5,4},{6,7},{7,6},{8,9},{9,8},{10,11... | collective-permute-start | bytes 1966088 | tf_op jit(solution)/shard_map/ppermute | solution.py:35
  47.3 10.4 %shard_map.91 = (f32[8,640,128]{2,1,0:T(8,128)}, f32[8,16,128]{2,1,0:T(8,128)}) custom-call(s32[8,32]{1,0:T(8,128)} %convert_element_type.3.mask_ref, bf16[256,640]{1,0:T(8,128)(2,1)} %refs_2_.5, bf16[256,640]{1,0:T(8,128)(2,1)} %copy-done.9, bf16[256,640]{1,0:T(8,128)(2,1)} %copy-done.10, bf16[256,640]{1,0:T(8,128)(2,1)} %copy-done.11, ...), custom_call_target="tpu_custom_call" | custom-call | flops 4000000000 | bytes 6291456 | tf_op jit(solution)/shard_map/pallas_call | solution.py:206
  60.4 2.7 %collective-permute-start.20 = (bf16[10,128,128]{2,1,0:T(8,128)(2,1)S(1)}, bf16[10,128,128]{2,1,0:T(8,128)(2,1)}, u32[]{:S(2)}, u32[]{:S(2)}) collective-permute-start(bf16[10,128,128]{2,1,0:T(8,128)(2,1)S(1)} %slice_bitcast_fusion), channel_id=1, source_target_pairs={{0,112},{16,0},{32,16},{48,32},{64,48},{80,64},{96,80},{112,96},{1... | collective-permute-start | bytes 983048 | tf_op jit(solution)/shard_map/ppermute | solution.py:26
  63.1 12.0 %shard_map.92 = (f32[8,640,128]{2,1,0:T(8,128)}, f32[8,16,128]{2,1,0:T(8,128)}) custom-call(s32[8,32]{1,0:T(8,128)} %convert_element_type.3.mask_ref, f32[8,640,128]{2,1,0:T(8,128)} %get-tuple-element.15.refs_0_, f32[8,16,128]{2,1,0:T(8,128)} %get-tuple-element.16.refs_1_, bf16[256,640]{1,0:T(8,128)(2,1)} %refs_2_.5, bf16[256,640]{1,0:T(8,128)(2,1)} %copy-done.9, ...), custom_call_target="tpu_custom_call" | custom-call | flops 4000000000 | bytes 4194304 | tf_op jit(solution)/shard_map/pallas_call | solution.py:206
  75.1 2.8 %collective-permute-start.33 = (bf16[256,1280]{1,0:T(8,128)(2,1)}, bf16[256,1280]{1,0:T(8,128)(2,1)S(1)}, u32[]{:S(2)}, u32[]{:S(2)}) collective-permute-start(bf16[256,1280]{1,0:T(8,128)(2,1)} %slice.26), channel_id=1, source_target_pairs={{0,12},{4,0},{8,4},{12,8},{1,13},{5,1},{9,5},{13,9},{2,14},{6,2},{... | collective-permute-start | bytes 1966088 | tf_op jit(solution)/shard_map/ppermute | solution.py:26
  79.2 12.5 %shard_map.93 = (f32[8,640,128]{2,1,0:T(8,128)}, f32[8,16,128]{2,1,0:T(8,128)}) custom-call(s32[8,32]{1,0:T(8,128)} %convert_element_type.3.mask_ref, f32[8,640,128]{2,1,0:T(8,128)} %get-tuple-element.17.refs_0_, f32[8,16,128]{2,1,0:T(8,128)} %get-tuple-element.18.refs_1_, bf16[256,640]{1,0:T(8,128)(2,1)} %refs_2_.5, bf16[256,640]{1,0:T(8,128)(2,1)} %copy-done.9, ...), custom_call_target="tpu_custom_call" | custom-call | flops 4000000000 | bytes 4194304 | tf_op jit(solution)/shard_map/pallas_call | solution.py:206
  92.4 8.8 %shard_map.94 = (bf16[2,672,128]{2,1,0:T(8,128)(2,1)}, bf16[2,672,128]{2,1,0:T(8,128)(2,1)}, bf16[2,672,128]{2,1,0:T(8,128)(2,1)}, bf16[2,672,128]{2,1,0:T(8,128)(2,1)}) custom-call(s32[8,32]{1,0:T(8,128)} %convert_element_type.3.mask_ref, f32[8,640,128]{2,1,0:T(8,128)} %get-tuple-element.19.refs_0_, f32[8,16,128]{2,1,0:T(8,128)} %get-tuple-element.20.refs_1_, ...), custom_call_target="tpu_custom_call" | custom-call | flops 4000000000 | bytes 2097152 | tf_op jit(solution)/shard_map/pallas_call | solution.py:206
  101.4 3.0 %collective-permute-start.24 = (bf16[2,672,128]{2,1,0:T(8,128)(2,1)}, bf16[2,672,128]{2,1,0:T(8,128)(2,1)}, u32[]{:S(2)}, u32[]{:S(2)}) collective-permute-start(bf16[2,672,128]{2,1,0:T(8,128)(2,1)} %get-tuple-element.23), channel_id=1, source_target_pairs={{0,2},{128,130},{2,0},{130,128},{1,3},{129,131},{3,1},{131,129},{4... | collective-permute-start | bytes 1032200 | tf_op jit(solution)/shard_map/ppermute | solution.py:31
  105.2 2.6 %collective-permute-start.35 = (bf16[384,1280]{1,0:T(8,128)(2,1)S(1)}, bf16[384,1280]{1,0:T(8,128)(2,1)S(1)}, u32[]{:S(2)}, u32[]{:S(2)}) collective-permute-start(bf16[384,1280]{1,0:T(8,128)(2,1)S(1)} %slice.25), channel_id=1, source_target_pairs={{0,12},{4,0},{8,4},{12,8},{1,13},{5,1},{9,5},{13,9},{2,14},{6,2},{... | collective-permute-start | bytes 2949128 | tf_op jit(solution)/shard_map/ppermute | solution.py:26
  107.8 3.9 %collective-permute-done.23.one = bf16[2,672,128]{2,1,0:T(8,128)(2,1)S(1)} collective-permute-done((bf16[2,672,128]{2,1,0:T(8,128)(2,1)}, bf16[2,672,128]{2,1,0:T(8,128)(2,1)S(1)}, u32[]{:S(2)}, u32[]{:S(2)}) %collective-permute-start.23) | collective-permute-done | bytes 344096 | tf_op jit(solution)/shard_map/ppermute | solution.py:31
  111.7 1.4 collective-permute-done.24.two
  113.1 2.6 %collective-permute-start.34 = (bf16[256,1280]{1,0:T(8,128)(2,1)}, bf16[256,1280]{1,0:T(8,128)(2,1)}, u32[]{:S(2)}, u32[]{:S(2)}) collective-permute-start(bf16[256,1280]{1,0:T(8,128)(2,1)} %copy-done.2), channel_id=1, source_target_pairs={{0,12},{4,0},{8,4},{12,8},{1,13},{5,1},{9,5},{13,9},{2,14},{6,2},{... | collective-permute-start | bytes 1966088 | tf_op jit(solution)/shard_map/ppermute | solution.py:26
  115.7 4.7 %collective-permute-done.25.three = bf16[2,672,128]{2,1,0:T(8,128)(2,1)} collective-permute-done((bf16[2,672,128]{2,1,0:T(8,128)(2,1)}, bf16[2,672,128]{2,1,0:T(8,128)(2,1)}, u32[]{:S(2)}, u32[]{:S(2)}) %collective-permute-start.25) | collective-permute-done | bytes 344096 | tf_op jit(solution)/shard_map/ppermute | solution.py:31
  120.4 2.4 %combine.1 = bf16[256,640]{1,0:T(8,128)(2,1)} custom-call(bf16[2,672,128]{2,1,0:T(8,128)(2,1)} %get-tuple-element.21.own, bf16[2,672,128]{2,1,0:T(8,128)(2,1)} %copy-done.3, bf16[2,672,128]{2,1,0:T(8,128)(2,1)} %collective-permute-done.24.two, bf16[2,672,128]{2,1,0:T(8,128)(2,1)} %collective-permute-done.25.three), custom_call_target="tpu_custom_call" | custom-call | tf_op jit(solution)/shard_map/combine/pallas_call | solution.py:242
  122.8 3.7 %collective-permute-start.26 = (bf16[256,640]{1,0:T(8,128)(2,1)}, bf16[256,640]{1,0:T(8,128)(2,1)S(1)}, u32[]{:S(2)}, u32[]{:S(2)}) collective-permute-start(bf16[256,640]{1,0:T(8,128)(2,1)} %combine.1), channel_id=1, source_target_pairs={{0,0},{1,4},{2,8},{3,12},{4,1},{5,5},{6,9},{7,13},{8,2},{9,6},{10,... | collective-permute-start | bytes 983048 | tf_op jit(solution)/shard_map/ppermute | solution.py:330
  126.5 3.5 %collective-permute-start.27 = (bf16[256,640]{1,0:T(8,128)(2,1)}, bf16[256,640]{1,0:T(8,128)(2,1)}, u32[]{:S(2)}, u32[]{:S(2)}) collective-permute-start(bf16[256,640]{1,0:T(8,128)(2,1)} %combine.1), channel_id=1, source_target_pairs={{0,2},{1,6},{2,10},{3,14},{4,3},{5,7},{6,11},{7,15},{8,0},{9,4},{1... | collective-permute-start | bytes 983048 | tf_op jit(solution)/shard_map/ppermute | solution.py:331
  130.0 19.8 %collective-permute-done.26.a = bf16[256,640]{1,0:T(8,128)(2,1)S(1)} collective-permute-done((bf16[256,640]{1,0:T(8,128)(2,1)}, bf16[256,640]{1,0:T(8,128)(2,1)S(1)}, u32[]{:S(2)}, u32[]{:S(2)}) %collective-permute-start.26) | collective-permute-done | bytes 327712 | tf_op jit(solution)/shard_map/ppermute | solution.py:330
  152.5 6.4 %project.1 = bf16[256,1280]{1,0:T(8,128)(2,1)} custom-call(s32[4]{0:T(128)} %and_select_fusion.1.place_ref, bf16[256,640]{1,0:T(8,128)(2,1)} %copy-done.4, bf16[256,640]{1,0:T(8,128)(2,1)} %collective-permute-done.27.b, bf16[256,640]{1,0:T(8,128)(2,1)} %collective-permute-done.28.c, bf16[256,640]{1,0:T(8,128)(2,1)} %collective-permute-done.29.d, ...), custom_call_target="tpu_custom_call" | custom-call | tf_op jit(solution)/shard_map/project/pallas_call | solution.py:265
  (93 shorter events, 18.1 us)
Async XLA Ops:
  2.1 21.0 %collective-permute-start.7 = (bf16[2,10,128,128]{3,2,1,0:T(8,128)(2,1)}, bf16[2,10,128,128]{3,2,1,0:T(8,128)(2,1)S(1)}, u32[]{:S(2)}, u32[]{:S(2)}) collective-permute-start(bf16[2,10,128,128]{3,2,1,0:T(8,128)(2,1)} %prepare.1.refs_4_), channel_id=1, source_target_pairs={{0,16},{16,32},{32,48},{48,64},{64,80},{80,96},{96,112},{112,0},{1... | collective-permute-start | bytes 1966088 | tf_op jit(solution)/shard_map/ppermute | solution.py:26
  4.5 18.6 %collective-permute-start.9 = (bf16[2,10,128,128]{3,2,1,0:T(8,128)(2,1)}, bf16[2,10,128,128]{3,2,1,0:T(8,128)(2,1)S(1)}, u32[]{:S(2)}, u32[]{:S(2)}) collective-permute-start(bf16[2,10,128,128]{3,2,1,0:T(8,128)(2,1)} %prepare.1.refs_4_), channel_id=1, source_target_pairs={{0,112},{16,0},{32,16},{48,32},{64,48},{80,64},{96,80},{112,96},{1... | collective-permute-start | bytes 1966088 | tf_op jit(solution)/shard_map/ppermute | solution.py:26
  13.0 4.6 %collective-permute-start = (s32[2,17]{1,0:T(2,128)S(1)}, s32[2,17]{1,0:T(2,128)S(1)}, u32[]{:S(2)}, u32[]{:S(2)}) collective-permute-start(s32[2,17]{1,0:T(2,128)S(1)} %pad_add_fusion.1), channel_id=1, source_target_pairs={{0,128},{128,2},{2,130},{130,0},{1,129},{129,3},{3,131},{131,1},{4... | collective-permute-start | bytes 416 | tf_op jit(solution)/shard_map/ppermute | solution.py:31
  13.6 12.9 %collective-permute-start.3 = (bf16[256,640]{1,0:T(8,128)(2,1)}, bf16[256,640]{1,0:T(8,128)(2,1)S(1)}, u32[]{:S(2)}, u32[]{:S(2)}) collective-permute-start(bf16[256,640]{1,0:T(8,128)(2,1)} %refs_2_.5), channel_id=1, source_target_pairs={{0,128},{128,2},{2,130},{130,0},{1,129},{129,3},{3,131},{131,1},{4... | collective-permute-start | bytes 983048 | tf_op jit(solution)/shard_map/ppermute | solution.py:31
  16.4 14.4 %collective-permute-start.4 = (bf16[256,640]{1,0:T(8,128)(2,1)}, bf16[256,640]{1,0:T(8,128)(2,1)S(1)}, u32[]{:S(2)}, u32[]{:S(2)}) collective-permute-start(bf16[256,640]{1,0:T(8,128)(2,1)} %refs_2_.5), channel_id=1, source_target_pairs={{0,2},{128,130},{2,0},{130,128},{1,3},{129,131},{3,1},{131,129},{4... | collective-permute-start | bytes 983048 | tf_op jit(solution)/shard_map/ppermute | solution.py:31
  17.6 15.9 %collective-permute-start.5 = (bf16[256,640]{1,0:T(8,128)(2,1)}, bf16[256,640]{1,0:T(8,128)(2,1)S(1)}, u32[]{:S(2)}, u32[]{:S(2)}) collective-permute-start(bf16[256,640]{1,0:T(8,128)(2,1)} %refs_2_.5), channel_id=1, source_target_pairs={{0,130},{128,0},{2,128},{130,2},{1,131},{129,1},{3,129},{131,3},{4... | collective-permute-start | bytes 983048 | tf_op jit(solution)/shard_map/ppermute | solution.py:31
  23.1 16.4 %collective-permute-start.11 = (bf16[2,10,128,128]{3,2,1,0:T(8,128)(2,1)S(1)}, bf16[2,10,128,128]{3,2,1,0:T(8,128)(2,1)}, u32[]{:S(2)}, u32[]{:S(2)}) collective-permute-start(bf16[2,10,128,128]{3,2,1,0:T(8,128)(2,1)S(1)} %collective-permute-done.7.refs_6_), channel_id=1, source_target_pairs={{0,16},{16,32},{32,48},{48,64},{64,80},{80,96},{96,112},{112,0},{1... | collective-permute-start | bytes 1966088 | tf_op jit(solution)/shard_map/ppermute | solution.py:26
  23.1 16.3 %collective-permute-start.13 = (bf16[2,10,128,128]{3,2,1,0:T(8,128)(2,1)S(1)}, bf16[2,10,128,128]{3,2,1,0:T(8,128)(2,1)}, u32[]{:S(2)}, u32[]{:S(2)}) collective-permute-start(bf16[2,10,128,128]{3,2,1,0:T(8,128)(2,1)S(1)} %collective-permute-done.9.refs_8_), channel_id=1, source_target_pairs={{0,112},{16,0},{32,16},{48,32},{64,48},{80,64},{96,80},{112,96},{1... | collective-permute-start | bytes 1966088 | tf_op jit(solution)/shard_map/ppermute | solution.py:26
  26.5 16.4 %collective-permute-start.6 = (bf16[2,10,128,128]{3,2,1,0:T(8,128)(2,1)}, bf16[2,10,128,128]{3,2,1,0:T(8,128)(2,1)}, u32[]{:S(2)}, u32[]{:S(2)}) collective-permute-start(bf16[2,10,128,128]{3,2,1,0:T(8,128)(2,1)} %prepare.1.refs_4_), channel_id=1, source_target_pairs={{0,1},{1,0},{2,3},{3,2},{4,5},{5,4},{6,7},{7,6},{8,9},{9,8},{10,11... | collective-permute-start | bytes 1966088 | tf_op jit(solution)/shard_map/ppermute | solution.py:35
  30.8 13.5 %collective-permute-start.8 = (bf16[2,10,128,128]{3,2,1,0:T(8,128)(2,1)S(1)}, bf16[2,10,128,128]{3,2,1,0:T(8,128)(2,1)}, u32[]{:S(2)}, u32[]{:S(2)}) collective-permute-start(bf16[2,10,128,128]{3,2,1,0:T(8,128)(2,1)S(1)} %collective-permute-done.7.refs_6_), channel_id=1, source_target_pairs={{0,1},{1,0},{2,3},{3,2},{4,5},{5,4},{6,7},{7,6},{8,9},{9,8},{10,11... | collective-permute-start | bytes 1966088 | tf_op jit(solution)/shard_map/ppermute | solution.py:35
  33.5 13.7 %collective-permute-start.10 = (bf16[2,10,128,128]{3,2,1,0:T(8,128)(2,1)S(1)}, bf16[2,10,128,128]{3,2,1,0:T(8,128)(2,1)}, u32[]{:S(2)}, u32[]{:S(2)}) collective-permute-start(bf16[2,10,128,128]{3,2,1,0:T(8,128)(2,1)S(1)} %collective-permute-done.9.refs_8_), channel_id=1, source_target_pairs={{0,1},{1,0},{2,3},{3,2},{4,5},{5,4},{6,7},{7,6},{8,9},{9,8},{10,11... | collective-permute-start | bytes 1966088 | tf_op jit(solution)/shard_map/ppermute | solution.py:35
  39.5 18.2 %collective-permute-start.15 = (bf16[2,10,128,128]{3,2,1,0:T(8,128)(2,1)}, bf16[2,10,128,128]{3,2,1,0:T(8,128)(2,1)}, u32[]{:S(2)}, u32[]{:S(2)}) collective-permute-start(bf16[2,10,128,128]{3,2,1,0:T(8,128)(2,1)} %collective-permute-done.11.refs_6_), channel_id=1, source_target_pairs={{0,16},{16,32},{32,48},{48,64},{64,80},{80,96},{96,112},{112,0},{1... | collective-permute-start | bytes 1966088 | tf_op jit(solution)/shard_map/ppermute | solution.py:26
  39.5 18.7 %collective-permute-start.17 = (bf16[2,10,128,128]{3,2,1,0:T(8,128)(2,1)}, bf16[2,10,128,128]{3,2,1,0:T(8,128)(2,1)}, u32[]{:S(2)}, u32[]{:S(2)}) collective-permute-start(bf16[2,10,128,128]{3,2,1,0:T(8,128)(2,1)} %collective-permute-done.13.refs_8_), channel_id=1, source_target_pairs={{0,112},{16,0},{32,16},{48,32},{64,48},{80,64},{96,80},{112,96},{1... | collective-permute-start | bytes 1966088 | tf_op jit(solution)/shard_map/ppermute | solution.py:26
  42.9 62.3 %collective-permute-start.30 = (bf16[384,1280]{1,0:T(8,128)(2,1)S(1)}, bf16[384,1280]{1,0:T(8,128)(2,1)S(1)}, u32[]{:S(2)}, u32[]{:S(2)}) collective-permute-start(bf16[384,1280]{1,0:T(8,128)(2,1)S(1)} %slice.25), channel_id=1, source_target_pairs={{0,4},{4,8},{8,12},{12,0},{1,5},{5,9},{9,13},{13,1},{2,6},{6,10},{... | collective-permute-start | bytes 2949128 | tf_op jit(solution)/shard_map/ppermute | solution.py:26
  44.2 16.1 %collective-permute-start.12 = (bf16[2,10,128,128]{3,2,1,0:T(8,128)(2,1)}, bf16[2,10,128,128]{3,2,1,0:T(8,128)(2,1)}, u32[]{:S(2)}, u32[]{:S(2)}) collective-permute-start(bf16[2,10,128,128]{3,2,1,0:T(8,128)(2,1)} %collective-permute-done.11.refs_6_), channel_id=1, source_target_pairs={{0,1},{1,0},{2,3},{3,2},{4,5},{5,4},{6,7},{7,6},{8,9},{9,8},{10,11... | collective-permute-start | bytes 1966088 | tf_op jit(solution)/shard_map/ppermute | solution.py:35
  47.2 13.2 %collective-permute-start.14 = (bf16[2,10,128,128]{3,2,1,0:T(8,128)(2,1)}, bf16[2,10,128,128]{3,2,1,0:T(8,128)(2,1)}, u32[]{:S(2)}, u32[]{:S(2)}) collective-permute-start(bf16[2,10,128,128]{3,2,1,0:T(8,128)(2,1)} %collective-permute-done.13.refs_8_), channel_id=1, source_target_pairs={{0,1},{1,0},{2,3},{3,2},{4,5},{5,4},{6,7},{7,6},{8,9},{9,8},{10,11... | collective-permute-start | bytes 1966088 | tf_op jit(solution)/shard_map/ppermute | solution.py:35
  57.7 21.4 %collective-permute-start.16 = (bf16[2,10,128,128]{3,2,1,0:T(8,128)(2,1)}, bf16[2,10,128,128]{3,2,1,0:T(8,128)(2,1)}, u32[]{:S(2)}, u32[]{:S(2)}) collective-permute-start(bf16[2,10,128,128]{3,2,1,0:T(8,128)(2,1)} %collective-permute-done.15.refs_6_), channel_id=1, source_target_pairs={{0,1},{1,0},{2,3},{3,2},{4,5},{5,4},{6,7},{7,6},{8,9},{9,8},{10,11... | collective-permute-start | bytes 1966088 | tf_op jit(solution)/shard_map/ppermute | solution.py:35
  58.2 21.0 %collective-permute-start.18 = (bf16[2,10,128,128]{3,2,1,0:T(8,128)(2,1)}, bf16[2,10,128,128]{3,2,1,0:T(8,128)(2,1)}, u32[]{:S(2)}, u32[]{:S(2)}) collective-permute-start(bf16[2,10,128,128]{3,2,1,0:T(8,128)(2,1)} %collective-permute-done.17.refs_8_), channel_id=1, source_target_pairs={{0,1},{1,0},{2,3},{3,2},{4,5},{5,4},{6,7},{7,6},{8,9},{9,8},{10,11... | collective-permute-start | bytes 1966088 | tf_op jit(solution)/shard_map/ppermute | solution.py:35
  60.3 14.8 %collective-permute-start.19 = (bf16[10,128,128]{2,1,0:T(8,128)(2,1)S(1)}, bf16[10,128,128]{2,1,0:T(8,128)(2,1)S(1)}, u32[]{:S(2)}, u32[]{:S(2)}) collective-permute-start(bf16[10,128,128]{2,1,0:T(8,128)(2,1)S(1)} %slice_bitcast_fusion.1), channel_id=1, source_target_pairs={{0,16},{16,32},{32,48},{48,64},{64,80},{80,96},{96,112},{112,0},{1... | collective-permute-start | bytes 983048 | tf_op jit(solution)/shard_map/ppermute | solution.py:26
  60.4 17.4 %collective-permute-start.20 = (bf16[10,128,128]{2,1,0:T(8,128)(2,1)S(1)}, bf16[10,128,128]{2,1,0:T(8,128)(2,1)}, u32[]{:S(2)}, u32[]{:S(2)}) collective-permute-start(bf16[10,128,128]{2,1,0:T(8,128)(2,1)S(1)} %slice_bitcast_fusion), channel_id=1, source_target_pairs={{0,112},{16,0},{32,16},{48,32},{64,48},{80,64},{96,80},{112,96},{1... | collective-permute-start | bytes 983048 | tf_op jit(solution)/shard_map/ppermute | solution.py:26
  75.1 29.3 %collective-permute-start.33 = (bf16[256,1280]{1,0:T(8,128)(2,1)}, bf16[256,1280]{1,0:T(8,128)(2,1)S(1)}, u32[]{:S(2)}, u32[]{:S(2)}) collective-permute-start(bf16[256,1280]{1,0:T(8,128)(2,1)} %slice.26), channel_id=1, source_target_pairs={{0,12},{4,0},{8,4},{12,8},{1,13},{5,1},{9,5},{13,9},{2,14},{6,2},{... | collective-permute-start | bytes 1966088 | tf_op jit(solution)/shard_map/ppermute | solution.py:26
  77.9 13.8 %collective-permute-start.21 = (bf16[10,128,128]{2,1,0:T(8,128)(2,1)S(1)}, bf16[10,128,128]{2,1,0:T(8,128)(2,1)S(1)}, u32[]{:S(2)}, u32[]{:S(2)}) collective-permute-start(bf16[10,128,128]{2,1,0:T(8,128)(2,1)S(1)} %collective-permute-done.19.refs_6_), channel_id=1, source_target_pairs={{0,1},{1,0},{2,3},{3,2},{4,5},{5,4},{6,7},{7,6},{8,9},{9,8},{10,11... | collective-permute-start | bytes 983048 | tf_op jit(solution)/shard_map/ppermute | solution.py:35
  79.1 12.6 %collective-permute-start.22 = (bf16[10,128,128]{2,1,0:T(8,128)(2,1)}, bf16[10,128,128]{2,1,0:T(8,128)(2,1)}, u32[]{:S(2)}, u32[]{:S(2)}) collective-permute-start(bf16[10,128,128]{2,1,0:T(8,128)(2,1)} %collective-permute-done.20.refs_7_), channel_id=1, source_target_pairs={{0,1},{1,0},{2,3},{3,2},{4,5},{5,4},{6,7},{7,6},{8,9},{9,8},{10,11... | collective-permute-start | bytes 983048 | tf_op jit(solution)/shard_map/ppermute | solution.py:35
  101.2 10.5 %collective-permute-start.23 = (bf16[2,672,128]{2,1,0:T(8,128)(2,1)}, bf16[2,672,128]{2,1,0:T(8,128)(2,1)S(1)}, u32[]{:S(2)}, u32[]{:S(2)}) collective-permute-start(bf16[2,672,128]{2,1,0:T(8,128)(2,1)} %get-tuple-element.22), channel_id=1, source_target_pairs={{0,130},{128,0},{2,128},{130,2},{1,131},{129,1},{3,129},{131,3},{4... | collective-permute-start | bytes 1032200 | tf_op jit(solution)/shard_map/ppermute | solution.py:31
  101.3 25.2 %collective-permute-start.31 = (bf16[256,1280]{1,0:T(8,128)(2,1)}, bf16[256,1280]{1,0:T(8,128)(2,1)}, u32[]{:S(2)}, u32[]{:S(2)}) collective-permute-start(bf16[256,1280]{1,0:T(8,128)(2,1)} %slice.26), channel_id=1, source_target_pairs={{0,4},{4,8},{8,12},{12,0},{1,5},{5,9},{9,13},{13,1},{2,6},{6,10},{... | collective-permute-start | bytes 1966088 | tf_op jit(solution)/shard_map/ppermute | solution.py:26
  101.4 11.7 %collective-permute-start.24 = (bf16[2,672,128]{2,1,0:T(8,128)(2,1)}, bf16[2,672,128]{2,1,0:T(8,128)(2,1)}, u32[]{:S(2)}, u32[]{:S(2)}) collective-permute-start(bf16[2,672,128]{2,1,0:T(8,128)(2,1)} %get-tuple-element.23), channel_id=1, source_target_pairs={{0,2},{128,130},{2,0},{130,128},{1,3},{129,131},{3,1},{131,129},{4... | collective-permute-start | bytes 1032200 | tf_op jit(solution)/shard_map/ppermute | solution.py:31
  104.3 16.0 %collective-permute-start.25 = (bf16[2,672,128]{2,1,0:T(8,128)(2,1)}, bf16[2,672,128]{2,1,0:T(8,128)(2,1)}, u32[]{:S(2)}, u32[]{:S(2)}) collective-permute-start(bf16[2,672,128]{2,1,0:T(8,128)(2,1)} %get-tuple-element.24), channel_id=1, source_target_pairs={{0,128},{128,2},{2,130},{130,0},{1,129},{129,3},{3,131},{131,1},{4... | collective-permute-start | bytes 1032200 | tf_op jit(solution)/shard_map/ppermute | solution.py:31
  105.2 46.3 %collective-permute-start.35 = (bf16[384,1280]{1,0:T(8,128)(2,1)S(1)}, bf16[384,1280]{1,0:T(8,128)(2,1)S(1)}, u32[]{:S(2)}, u32[]{:S(2)}) collective-permute-start(bf16[384,1280]{1,0:T(8,128)(2,1)S(1)} %slice.25), channel_id=1, source_target_pairs={{0,12},{4,0},{8,4},{12,8},{1,13},{5,1},{9,5},{13,9},{2,14},{6,2},{... | collective-permute-start | bytes 2949128 | tf_op jit(solution)/shard_map/ppermute | solution.py:26
  111.7 39.8 %collective-permute-start.32 = (bf16[384,1280]{1,0:T(8,128)(2,1)S(1)}, bf16[384,1280]{1,0:T(8,128)(2,1)}, u32[]{:S(2)}, u32[]{:S(2)}) collective-permute-start(bf16[384,1280]{1,0:T(8,128)(2,1)S(1)} %collective-permute-done.30.t1), channel_id=1, source_target_pairs={{0,4},{4,8},{8,12},{12,0},{1,5},{5,9},{9,13},{13,1},{2,6},{6,10},{... | collective-permute-start | bytes 2949128 | tf_op jit(solution)/shard_map/ppermute | solution.py:26
  113.1 38.4 %collective-permute-start.34 = (bf16[256,1280]{1,0:T(8,128)(2,1)}, bf16[256,1280]{1,0:T(8,128)(2,1)}, u32[]{:S(2)}, u32[]{:S(2)}) collective-permute-start(bf16[256,1280]{1,0:T(8,128)(2,1)} %copy-done.2), channel_id=1, source_target_pairs={{0,12},{4,0},{8,4},{12,8},{1,13},{5,1},{9,5},{13,9},{2,14},{6,2},{... | collective-permute-start | bytes 1966088 | tf_op jit(solution)/shard_map/ppermute | solution.py:26
  122.8 27.0 %collective-permute-start.26 = (bf16[256,640]{1,0:T(8,128)(2,1)}, bf16[256,640]{1,0:T(8,128)(2,1)S(1)}, u32[]{:S(2)}, u32[]{:S(2)}) collective-permute-start(bf16[256,640]{1,0:T(8,128)(2,1)} %combine.1), channel_id=1, source_target_pairs={{0,0},{1,4},{2,8},{3,12},{4,1},{5,5},{6,9},{7,13},{8,2},{9,6},{10,... | collective-permute-start | bytes 983048 | tf_op jit(solution)/shard_map/ppermute | solution.py:330
  126.5 23.2 %collective-permute-start.27 = (bf16[256,640]{1,0:T(8,128)(2,1)}, bf16[256,640]{1,0:T(8,128)(2,1)}, u32[]{:S(2)}, u32[]{:S(2)}) collective-permute-start(bf16[256,640]{1,0:T(8,128)(2,1)} %combine.1), channel_id=1, source_target_pairs={{0,2},{1,6},{2,10},{3,14},{4,3},{5,7},{6,11},{7,15},{8,0},{9,4},{1... | collective-permute-start | bytes 983048 | tf_op jit(solution)/shard_map/ppermute | solution.py:331
  (18 other events, 252.1 us)
where the time goes:
time: 160 us; the launch traced here: 159 us
  Pallas kernels  54.4 us (34%)
  starting transfers between devices  51.6 us (32%)
  waiting for transfers between devices  40.7 us (25%)
  local copies, waits for them, and re-layouts  8.86 us (6%)
  other arithmetic  3 us (2%)
    pallas_call x4, Pallas kernels, attend(): pl.pallas_call(functools.partial(attention, first_pair, pairs, split, sta...  43.6 us
    ppermute x14, starting transfers between devices, shift(): lax.ppermute(value, axes, [(i, (i + steps) % size) for i in range(size)])  23.8 us
    ppermute x1, waiting for transfers between devices, stages(): lax.ppermute(attended, ('y', 'xhi', 'core'), [(4 * i + j, 4 * j + i) for...  19.8 us
    ppermute x9, waiting for transfers between devices, shift_x(): lax.ppermute(value, ('xlo', 'xhi'), [(at[x], at[(x + steps) % 4]) for x i...  13.7 us
    ppermute x9, starting transfers between devices, shift_x(): lax.ppermute(value, ('xlo', 'xhi'), [(at[x], at[(x + steps) % 4]) for x i...  10.5 us
    ppermute x11, starting transfers between devices, swap_core(): return lax.ppermute(value, 'core', [(0, 1), (1, 0)])  10.1 us
    ppermute x14, waiting for transfers between devices, shift(): lax.ppermute(value, axes, [(i, (i + steps) % size) for i in range(size)])  6.7 us
    pallas_call x1, Pallas kernels, project(): pl.pallas_call(project_kernel, in_specs=[pl.BlockSpec(memory_space=pltpu....  6.36 us
  transfers between devices with their start and end apart: 36, of which 9 were waited for; matrix products, arithmetic and copies ran while one was open for 6% of the time, Pallas kernels for 29%

commit v1 on v0

v1 whole, which is shorter than its diff:
```python
import functools
import math

import jax
import jax.numpy as jnp
from jax import lax
from jax.experimental import pallas as pl
from jax.experimental.pallas import tpu as pltpu
from jax.sharding import Mesh, PartitionSpec as P


HD = 128
BLOCK = 128
LIST = 16
HEADS = 5
ROWS = 2 * BLOCK
WIDTH = HEADS * HD
TAIL = 32
EMPTY = -1e30
SCALE2 = math.log2(math.e) / HD**0.5

SOURCES = [(0, 0), (0, 1)] + [(s * d, c) for d in (1, 2, 3) for s in (-1, 1) for c in (0, 1)] + [(4, 0), (4, 1)]


def shift(value, axes, size, steps):
    return lax.ppermute(value, axes, [(i, (i + steps) % size) for i in range(size)])


def shift_x(value, steps):
    at = [2 * (x % 2) + x // 2 for x in range(4)]
    return lax.ppermute(value, ("xlo", "xhi"), [(at[x], at[(x + steps) % 4]) for x in range(4)])


def swap_core(value):
    return lax.ppermute(value, "core", [(0, 1), (1, 0)])


def prepare_kernel(keys, values, out):
    for b in range(2):
        rows = slice(b * BLOCK, (b + 1) * BLOCK)
        for h in range(HEADS):
            cols = slice(h * HD, (h + 1) * HD)
            out[0, b * HEADS + h] = keys[rows, cols]
            out[1, b * HEADS + h] = values[rows, cols].T


def prepare(keys, values):
    return pl.pallas_call(
        prepare_kernel,
        out_shape=jax.ShapeDtypeStruct((2, 2 * HEADS, BLOCK, HD), jnp.bfloat16),
        name="prepare",
    )(keys, values)


def attention(first_pair, pairs, split, start, last, heads, mask_ref, *refs):
    refs = list(refs)
    if not start:
        acc_in, ml_in = refs[:2]
        refs = refs[2:]
    sent, refs = refs[:4], refs[4:]
    count = pairs * 2 if split else pairs
    sources, refs = refs[:count], refs[count:]
    outs, refs = (refs[:4], refs[4:]) if last else (refs[:2], refs[2:])
    q, kv, acc, sems, scores, tops, totals, ml, slots, blocks, counts = refs[:11]
    size = len(heads)
    height = size * HD

    copies = []
    for i, source in enumerate(sources):
        target = kv.at[i // 2, i % 2] if split else kv.at[i]
        copies.append(pltpu.make_async_copy(source, target, sems.at[i]))
    for i, source in enumerate(sent):
        copies.append(pltpu.make_async_copy(source, q.at[i], sems.at[count + i]))
    for copy in copies:
        copy.start()
    if not start:
        state = pltpu.make_async_copy(
            acc_in.at[:, heads[0] * HD : heads[0] * HD + height, :], acc.at[0:8], sems.at[count + 4]
        )
        state.start()

    n = jnp.int32(0)
    for i in range(8):
        before = n
        for b in range(2 * pairs):
            slots[n] = jnp.int32(i)
            blocks[n] = jnp.int32(b)
            n = n + mask_ref[i, 2 * first_pair + b]
        counts[i] = n - before
    slots[n] = jnp.int32(8)
    blocks[n] = jnp.int32(0)
    trips = (n + 1) >> 1
    tops[...] = jnp.full(tops.shape, EMPTY, jnp.float32)
    totals[...] = jnp.zeros(totals.shape, jnp.float32)
    if start:
        acc[...] = jnp.zeros(acc.shape, jnp.float32)
    for copy in copies:
        copy.wait()

    def first_pass(j, carry):
        for u in range(2):
            i = 2 * j + u
            slot, b = slots[i], blocks[i]
            at = slot & 7
            pair, tile = b >> 1, (b & 1) * HEADS
            q_rows = pl.ds(pl.multiple_of((at & 1) * BLOCK, BLOCK), BLOCK)
            for k, h in enumerate(heads):
                s = (
                    lax.dot_general(
                        kv[pair, 0, tile + h],
                        q[at >> 1, q_rows, h * HD : (h + 1) * HD],
                        (((1,), (1,)), ((), ())),
                        preferred_element_type=jnp.float32,
                    )
                    * SCALE2
                )
                scores[i, k] = s
                tops[slot, k] = jnp.maximum(tops[slot, k], jnp.max(s.reshape(16, 8, BLOCK), axis=0))
        return carry

    lax.fori_loop(0, trips, first_pass, 0)
    if not start:
        state.wait()
    line = lax.broadcasted_iota(jnp.int32, (8, BLOCK), 0)

    def middle(i, carry):
        peak = jnp.full((8, BLOCK), EMPTY, jnp.float32) if start else ml_in[0, i]
        old = peak
        for k, h in enumerate(heads):
            top = jnp.max(tops[i, k], axis=0, keepdims=True)
            peak = jnp.where(line == h, jnp.maximum(peak, top), peak)
        ml[0, i] = peak
        if not start:
            factor = jnp.exp2(old - peak)
            ml[1, i] = ml_in[1, i] * factor

            @pl.when(counts[i] > 0)
            def _():
                for k, h in enumerate(heads):
                    rows = slice(k * HD, (k + 1) * HD)
                    acc[i, rows, :] = acc[i, rows, :] * factor[h : h + 1]

        return carry

    lax.fori_loop(0, 8, middle, 0)

    def second_pass(j, carry):
        for u in range(2):
            i = 2 * j + u
            slot, b = slots[i], blocks[i]
            pair, tile = b >> 1, (b & 1) * HEADS
            for k, h in enumerate(heads):
                rows = slice(k * HD, (k + 1) * HD)
                p = jnp.exp2(scores[i, k] - ml[0, slot, h : h + 1, :])
                totals[slot, k] = totals[slot, k] + jnp.sum(p.reshape(16, 8, BLOCK), axis=0)
                acc[slot, rows, :] = acc[slot, rows, :] + jnp.dot(
                    kv[pair, 1, tile + h], p.astype(jnp.bfloat16), preferred_element_type=jnp.float32
                )
        return carry

    lax.fori_loop(0, trips, second_pass, 0)

    if not last:
        acc_out, ml_out = outs
        leave = pltpu.make_async_copy(acc.at[0:8], acc_out, sems.at[count + 4])
        leave.start()

    def sums(i):
        weight = jnp.zeros((8, BLOCK), jnp.float32) if start else ml[1, i]
        for k, h in enumerate(heads):
            total = jnp.sum(totals[i, k], axis=0, keepdims=True)
            weight = jnp.where(line == h, weight + total, weight)
        return weight

    if not last:

        def finish(i, carry):
            ml_out[0, i] = ml[0, i]
            ml_out[1, i] = sums(i)
            return carry

        lax.fori_loop(0, 8, finish, 0)
        leave.wait()
        return

    part, out_sems = refs[11:]
    leaves = []
    for r in range(4):
        for i in (2 * r, 2 * r + 1):
            weight = sums(i)
            some = weight > 0.0
            weight = jnp.where(some, weight, 1.0)
            lse = jnp.where(some, ml[0, i] + jnp.log2(weight), EMPTY)
            scale = 1.0 / weight
            for k, h in enumerate(heads):
                rows = slice(k * HD, (k + 1) * HD)
                part[i, rows, :] = (acc[i, rows, :] * scale[h : h + 1]).astype(jnp.bfloat16)
            tables = []
            for _ in range(3):
                piece = lse.astype(jnp.bfloat16).astype(jnp.float32)
                tables.append(piece)
                lse = lse - piece
            tables.append(jnp.zeros((8, BLOCK), jnp.float32))
            part[i, height : height + TAIL, :] = jnp.concatenate(tables, axis=0).astype(jnp.bfloat16)
        leaves.append(pltpu.make_async_copy(part.at[2 * r : 2 * r + 2], outs[r], out_sems.at[r]))
        leaves[-1].start()
    for leave in leaves:
        leave.wait()


def attend(mask, queries, state, sources, first_pair, pairs, heads=None):
    start, last = state is None, heads is not None
    heads = heads or tuple(range(HEADS))
    split = len(sources) == 2 * pairs
    height = len(heads) * HD
    limit = 16 * pairs + 2
    scratch = [
        pltpu.VMEM((4, ROWS, WIDTH), jnp.bfloat16),
        pltpu.VMEM((pairs, 2, 2 * HEADS, BLOCK, HD), jnp.bfloat16),
        pltpu.VMEM((9, height, BLOCK), jnp.float32),
        pltpu.SemaphoreType.DMA((len(sources) + 5,)),
        pltpu.VMEM((limit, len(heads), BLOCK, BLOCK), jnp.float32),
        pltpu.VMEM((9, len(heads), 8, BLOCK), jnp.float32),
        pltpu.VMEM((9, len(heads), 8, BLOCK), jnp.float32),
        pltpu.VMEM((2, 9, 8, BLOCK), jnp.float32),
        pltpu.SMEM((limit,), jnp.int32),
        pltpu.SMEM((limit,), jnp.int32),
        pltpu.SMEM((8,), jnp.int32),
    ]
    anywhere = pl.BlockSpec(memory_space=pl.ANY)
    vmem = pl.BlockSpec(memory_space=pltpu.VMEM)
    if last:
        out_specs = [anywhere] * 4
        out_shape = [jax.ShapeDtypeStruct((2, height + TAIL, BLOCK), jnp.bfloat16)] * 4
        scratch += [pltpu.VMEM((8, height + TAIL, BLOCK), jnp.bfloat16), pltpu.SemaphoreType.DMA((4,))]
    else:
        out_specs = [anywhere, vmem]
        out_shape = [
            jax.ShapeDtypeStruct((8, WIDTH, BLOCK), jnp.float32),
            jax.ShapeDtypeStruct((2, 8, 8, BLOCK), jnp.float32),
        ]
    return pl.pallas_call(
        functools.partial(attention, first_pair, pairs, split, start, last, heads),
        in_specs=[pl.BlockSpec(memory_space=pltpu.SMEM)]
        + ([] if start else [anywhere, vmem])
        + [pl.BlockSpec(memory_space=pltpu.HBM)] * (4 + len(sources)),
        out_specs=out_specs,
        scratch_shapes=scratch,
        out_shape=out_shape,
        cost_estimate=pl.CostEstimate(
            flops=3 * 10**9, transcendentals=pairs * 4 * 5 * BLOCK**2, bytes_accessed=pairs * 2**20
        ),
        compiler_params=pltpu.CompilerParams(vmem_limit_bytes=56 * 2**20),
    )(mask, *(state or ()), *queries, *sources)


def combine_kernel(heads, own, one, two, three, out):
    parts = (own, one, two, three)
    height = len(heads) * HD
    for b in range(2):
        lses = []
        for part in parts:
            table = part[b, height : height + TAIL, :].astype(jnp.float32)
            lses.append(table[0:8] + table[8:16] + table[16:24])
        peak = functools.reduce(jnp.maximum, lses)
        shares = [jnp.exp2(lse - peak) for lse in lses]
        whole = 1.0 / (shares[0] + shares[1] + shares[2] + shares[3])
        shares = [share * whole for share in shares]
        for k, h in enumerate(heads):
            rows = slice(k * HD, (k + 1) * HD)
            value = parts[0][b, rows, :].astype(jnp.float32) * shares[0][h : h + 1]
            for part, share in zip(parts[1:], shares[1:]):
                value = value + part[b, rows, :].astype(jnp.float32) * share[h : h + 1]
            out[b * BLOCK : (b + 1) * BLOCK, rows] = value.T.astype(jnp.bfloat16)


def combine(parts, heads):
    return pl.pallas_call(
        functools.partial(combine_kernel, heads), out_shape=jax.ShapeDtypeStruct((ROWS, len(heads) * HD), jnp.bfloat16)
    )(*parts)


def project_kernel(place_ref, a, b, c, d, w0, w1, w2, w3, *refs):
    gate, sofar, out, rows = refs if len(refs) == 4 else (None, None, *refs)
    for j, piece in enumerate((a, b, c, d)):
        rows[place_ref[j]] = piece[...]
    for i in range(out.shape[1] // 256):
        cols = slice(i * 256, (i + 1) * 256)
        value = None if sofar is None else sofar[:, cols]
        for j, weight in enumerate((w0, w1, w2, w3)):
            new = jnp.dot(rows[j], weight[:, cols], preferred_element_type=jnp.float32)
            value = new if value is None else value + new
        if gate is not None:
            value = gate[:, cols] * value
        out[:, cols] = value.astype(out.dtype)


def project(place, pieces, weights, *more):
    cols = weights[0].shape[1]
    vmem = pl.BlockSpec(memory_space=pltpu.VMEM)
    return pl.pallas_call(
        project_kernel,
        in_specs=[pl.BlockSpec(memory_space=pltpu.SMEM)] + [vmem] * (8 + len(more)),
        out_specs=vmem,
        scratch_shapes=[pltpu.VMEM((4, *pieces[0].shape), jnp.bfloat16)],
        out_shape=jax.ShapeDtypeStruct((ROWS, cols), jnp.bfloat16 if more else jnp.float32),
        name="project" if more else "project_first",
    )(place, *pieces, *weights, *more)


HALVES = {"a": (0, 1, 2), "b": (3, 4)}
CUT = len(HALVES["a"]) * HD


def stages(queries, keys, values, block_lists, list_counts, out_weight, gate):
    xlo, z, y = lax.axis_index("xlo"), lax.axis_index("z"), lax.axis_index("y")
    xhi, core = lax.axis_index("xhi"), lax.axis_index("core")

    own = prepare(keys, values)
    before, after, near = [own], [own], [own]
    near.append(swap_core(own))
    for d in (1, 2, 3):
        before.append(shift(before[-1], "z", 8, 1))
        after.append(shift(after[-1], "z", 8, -1))
        near += [before[d], swap_core(before[d])]
        near += [after[d], swap_core(after[d])]
    far_keys = shift(before[3][0], "z", 8, 1)
    far_values = shift(after[3][1], "z", 8, -1)
    far = [far_keys, far_values, swap_core(far_keys)]
    far.append(swap_core(far_values))

    top, bottom = out_weight[:CUT], out_weight[CUT:]
    t1 = shift(top, "y", 4, 1)
    b3 = shift(bottom, "y", 4, -1)
    b1 = shift(bottom, "y", 4, 1)
    t3 = shift(top, "y", 4, -1)
    t2 = shift(t1, "y", 4, 1)
    b2 = shift(b3, "y", 4, -1)
    weights = {"a": [top, t1, t2, t3], "b": [bottom, b1, b2, b3]}

    table = jnp.concatenate([block_lists, list_counts[:, None]], axis=1)
    tables, all_queries = [table], [queries]
    for r in (1, 2, 3):
        tables.append(shift_x(table, r))
        all_queries.append(shift_x(queries, r))
    tables = jnp.stack(tables).reshape(8, LIST + 1)

    steps = jnp.array([s for s, _ in SOURCES], jnp.int32)
    other = jnp.array([c for _, c in SOURCES], jnp.int32)
    quarter = 2 * xhi + jnp.bitwise_xor(other, core)
    first = ((xlo * 8 + (z + steps) % 8) * 4 + quarter) * 2
    ids = (first[:, None] + jnp.arange(2)[None, :]).reshape(-1)
    used = jnp.arange(LIST)[None, :] < tables[:, LIST:]
    mask = jnp.any((tables[:, :LIST, None] == ids[None, None, :]) & used[:, :, None], axis=1).astype(jnp.int32)

    state = attend(mask, all_queries, None, near[:6], 0, 6)
    state = attend(mask, all_queries, state, near[6:10], 6, 4)
    state = attend(mask, all_queries, state, near[10:], 10, 4)
    places = [(i, j) for i in range(4) for j in range(4)]
    groups = jnp.stack([2 * xhi + core, 2 * (1 - xhi) + core, 2 * xhi + 1 - core, 2 * (1 - xhi) + 1 - core])
    place = ((y - groups) % 4).astype(jnp.int32)
    gate = gate[None, :]

    result = ()
    for name, heads in HALVES.items():
        parts = attend(mask, all_queries, state, far, 14, 2, heads)
        back = [parts[0]]
        for r in (1, 2, 3):
            back.append(shift_x(parts[r], -r))
        attended = combine(back, heads)
        here = lax.ppermute(attended, ("y", "xhi", "core"), [(4 * i + j, 4 * j + i) for i, j in places])
        there = lax.ppermute(attended, ("y", "xhi", "core"), [(4 * i + j, 4 * j + (i ^ 2)) for i, j in places])
        pieces = [here, there, swap_core(here)]
        pieces.append(swap_core(there))
        result = project(place, pieces, weights[name], *result)
        result = (gate, result)
    return result[1]


def solution(mesh):
    fine = Mesh(mesh.devices.reshape(2, 8, 4, 2, 2), ("xlo", "z", "y", "xhi", "core"))
    rows, rep = ("xlo", "z", "xhi", "core"), ("xhi", "core")
    placed = (P(rows, "y"), P(rows, "y"), P(rows, "y"), P(rows, None), P(rows), P("y", rep), P(rep))
    return jax.shard_map(stages, mesh=fine, in_specs=placed, out_specs=P(("xlo", "z", "y"), rep), check_vma=False)
```

time: 160 us -> 181 us (1.13)
  starting transfers between devices: 51.6 us -> 64.7 us
  waiting for transfers between devices: 40.7 us -> 53.2 us
  Pallas kernels: 54.4 us -> 50.2 us
    ppermute x14, waiting for transfers between devices: 6.7 us -> 31.3 us  [shift(): lax.ppermute(value, axes, [(i, (i + steps) % size) for i in range(size)])]
    ppermute x1 -> x2, waiting for transfers between devices: 19.8 us -> 4.28 us  [stages(): lax.ppermute(attended, ('y', 'xhi', 'core'), [(4 * i + j, 4 * j + i) for...]
    pallas_call x4 -> x5, Pallas kernels: 43.6 us -> 34.8 us  [attend(): pl.pallas_call(functools.partial(attention, first_pair, pairs, split, sta...]
    ppermute x1 -> x2, starting transfers between devices: 3.73 us -> 8.93 us  [stages(): lax.ppermute(attended, ('y', 'xhi', 'core'), [(4 * i + j, 4 * j + i) for...]
    ppermute x11 -> x13, starting transfers between devices: 10.1 us -> 14.7 us  [swap_core(): return lax.ppermute(value, 'core', [(0, 1), (1, 0)])]
    ppermute x9 -> x12, waiting for transfers between devices: 13.7 us -> 16.7 us  [shift_x(): lax.ppermute(value, ('xlo', 'xhi'), [(at[x], at[(x + steps) % 4]) for x i...]
    ppermute x9 -> x12, starting transfers between devices: 10.5 us -> 13.3 us  [shift_x(): lax.ppermute(value, ('xlo', 'xhi'), [(at[x], at[(x + steps) % 4]) for x i...]
    pallas_call x1 -> x2, Pallas kernels: 6.36 us -> 9.12 us  [project(): pl.pallas_call(project_kernel, in_specs=[pl.BlockSpec(memory_space=pltpu....]
  transfers between devices with their start and end apart: 36 -> 43, of which waited for: 9 -> 12; matrix products, arithmetic and copies ran while one was open for 6% -> 4% of each run, Pallas kernels for 29% -> 24%
where the time goes in v1:
time: 181 us; the launch traced here: 180 us
  starting transfers between devices  64.7 us (36%)
  waiting for transfers between devices  53.2 us (29%)
  Pallas kernels  50.2 us (28%)
  local copies, waits for them, and re-layouts  9.04 us (5%)
  other arithmetic  2.35 us (1%)
    pallas_call x5, Pallas kernels, attend(): pl.pallas_call(functools.partial(attention, first_pair, pairs, split, sta...  34.8 us
    ppermute x14, waiting for transfers between devices, shift(): lax.ppermute(value, axes, [(i, (i + steps) % size) for i in range(size)])  31.3 us
    ppermute x14, starting transfers between devices, shift(): lax.ppermute(value, axes, [(i, (i + steps) % size) for i in range(size)])  21.7 us
    ppermute x12, waiting for transfers between devices, shift_x(): lax.ppermute(value, ('xlo', 'xhi'), [(at[x], at[(x + steps) % 4]) for x i...  16.7 us
    ppermute x13, starting transfers between devices, swap_core(): return lax.ppermute(value, 'core', [(0, 1), (1, 0)])  14.7 us
    ppermute x12, starting transfers between devices, shift_x(): lax.ppermute(value, ('xlo', 'xhi'), [(at[x], at[(x + steps) % 4]) for x i...  13.3 us
    pallas_call x2, Pallas kernels, project(): pl.pallas_call(project_kernel, in_specs=[pl.BlockSpec(memory_space=pltpu....  9.12 us
    ppermute x2, starting transfers between devices, stages(): lax.ppermute(attended, ('y', 'xhi', 'core'), [(4 * i + j, 4 * j + i) for...  8.93 us
  transfers between devices with their start and end apart: 43, of which 12 were waited for; matrix products, arithmetic and copies ran while one was open for 4% of the time, Pallas kernels for 24%

profile of v1, /device:TPU:1, one launch (start us, length us, event | category | flops | bytes accessed | tf_op | source)
XLA Modules:
  0.0 179.9 jit_solution(2538026027017849716)
XLA Ops:
  2.1 2.5 %collective-permute-start.7 = (bf16[2,10,128,128]{3,2,1,0:T(8,128)(2,1)}, bf16[2,10,128,128]{3,2,1,0:T(8,128)(2,1)S(1)}, u32[]{:S(2)}, u32[]{:S(2)}) collective-permute-start(bf16[2,10,128,128]{3,2,1,0:T(8,128)(2,1)} %prepare.1.refs_4_), channel_id=1, source_target_pairs={{0,16},{16,32},{32,48},{48,64},{64,80},{80,96},{96,112},{112,0},{1... | collective-permute-start | bytes 1966088 | tf_op jit(solution)/shard_map/ppermute | solution.py:26
  4.6 3.9 %collective-permute-start.9 = (bf16[2,10,128,128]{3,2,1,0:T(8,128)(2,1)}, bf16[2,10,128,128]{3,2,1,0:T(8,128)(2,1)}, u32[]{:S(2)}, u32[]{:S(2)}) collective-permute-start(bf16[2,10,128,128]{3,2,1,0:T(8,128)(2,1)} %prepare.1.refs_4_), channel_id=1, source_target_pairs={{0,112},{16,0},{32,16},{48,32},{64,48},{80,64},{96,80},{112,96},{1... | collective-permute-start | bytes 1966088 | tf_op jit(solution)/shard_map/ppermute | solution.py:26
  8.5 14.6 %collective-permute-done.7.refs_6_ = bf16[2,10,128,128]{3,2,1,0:T(8,128)(2,1)S(1)} collective-permute-done((bf16[2,10,128,128]{3,2,1,0:T(8,128)(2,1)}, bf16[2,10,128,128]{3,2,1,0:T(8,128)(2,1)S(1)}, u32[]{:S(2)}, u32[]{:S(2)}) %collective-permute-start.7) | collective-permute-done | bytes 655392 | tf_op jit(solution)/shard_map/ppermute | solution.py:26
  23.2 2.7 %collective-permute-start.13 = (bf16[2,10,128,128]{3,2,1,0:T(8,128)(2,1)}, bf16[2,10,128,128]{3,2,1,0:T(8,128)(2,1)}, u32[]{:S(2)}, u32[]{:S(2)}) collective-permute-start(bf16[2,10,128,128]{3,2,1,0:T(8,128)(2,1)} %collective-permute-done.9.refs_8_), channel_id=1, source_target_pairs={{0,112},{16,0},{32,16},{48,32},{64,48},{80,64},{96,80},{112,96},{1... | collective-permute-start | bytes 1966088 | tf_op jit(solution)/shard_map/ppermute | solution.py:26
  27.0 2.5 %collective-permute-start.4 = (bf16[256,640]{1,0:T(8,128)(2,1)}, bf16[256,640]{1,0:T(8,128)(2,1)}, u32[]{:S(2)}, u32[]{:S(2)}) collective-permute-start(bf16[256,640]{1,0:T(8,128)(2,1)} %refs_2_.7), channel_id=1, source_target_pairs={{0,2},{128,130},{2,0},{130,128},{1,3},{129,131},{3,1},{131,129},{4... | collective-permute-start | bytes 983048 | tf_op jit(solution)/shard_map/ppermute | solution.py:31
  35.1 2.7 %collective-permute-start.1 = (s32[2,17]{1,0:T(2,128)S(1)}, s32[2,17]{1,0:T(2,128)S(1)}, u32[]{:S(2)}, u32[]{:S(2)}) collective-permute-start(s32[2,17]{1,0:T(2,128)S(1)} %pad_add_fusion.1), channel_id=1, source_target_pairs={{0,2},{128,130},{2,0},{130,128},{1,3},{129,131},{3,1},{131,129},{4... | collective-permute-start | bytes 416 | tf_op jit(solution)/shard_map/ppermute | solution.py:31
  37.9 5.0 %collective-permute-done.1 = s32[2,17]{1,0:T(2,128)S(1)} collective-permute-done((s32[2,17]{1,0:T(2,128)S(1)}, s32[2,17]{1,0:T(2,128)S(1)}, u32[]{:S(2)}, u32[]{:S(2)}) %collective-permute-start.1) | collective-permute-done | bytes 168 | tf_op jit(solution)/shard_map/ppermute | solution.py:31
  42.8 3.6 %collective-permute-done = s32[2,17]{1,0:T(2,128)S(1)} collective-permute-done((s32[2,17]{1,0:T(2,128)S(1)}, s32[2,17]{1,0:T(2,128)S(1)}, u32[]{:S(2)}, u32[]{:S(2)}) %collective-permute-start) | collective-permute-done | bytes 168 | tf_op jit(solution)/shard_map/ppermute | solution.py:31
  46.5 3.8 %collective-permute-start.6 = (bf16[2,10,128,128]{3,2,1,0:T(8,128)(2,1)}, bf16[2,10,128,128]{3,2,1,0:T(8,128)(2,1)}, u32[]{:S(2)}, u32[]{:S(2)}) collective-permute-start(bf16[2,10,128,128]{3,2,1,0:T(8,128)(2,1)} %prepare.1.refs_4_), channel_id=1, source_target_pairs={{0,1},{1,0},{2,3},{3,2},{4,5},{5,4},{6,7},{7,6},{8,9},{9,8},{10,11... | collective-permute-start | bytes 1966088 | tf_op jit(solution)/shard_map/ppermute | solution.py:35
  51.8 2.7 %collective-permute-start.17 = (bf16[2,10,128,128]{3,2,1,0:T(8,128)(2,1)}, bf16[2,10,128,128]{3,2,1,0:T(8,128)(2,1)}, u32[]{:S(2)}, u32[]{:S(2)}) collective-permute-start(bf16[2,10,128,128]{3,2,1,0:T(8,128)(2,1)} %collective-permute-done.13.refs_8_), channel_id=1, source_target_pairs={{0,112},{16,0},{32,16},{48,32},{64,48},{80,64},{96,80},{112,96},{1... | collective-permute-start | bytes 1966088 | tf_op jit(solution)/shard_map/ppermute | solution.py:26
  56.1 3.9 %collective-permute-done.5.refs_3_.refs_5_ = bf16[256,640]{1,0:T(8,128)(2,1)} collective-permute-done((bf16[256,640]{1,0:T(8,128)(2,1)}, bf16[256,640]{1,0:T(8,128)(2,1)}, u32[]{:S(2)}, u32[]{:S(2)}) %collective-permute-start.5) | collective-permute-done | bytes 327712 | tf_op jit(solution)/shard_map/ppermute | solution.py:31
  60.9 7.0 %collective-permute-done.15.refs_6_ = bf16[2,10,128,128]{3,2,1,0:T(8,128)(2,1)S(1)} collective-permute-done((bf16[2,10,128,128]{3,2,1,0:T(8,128)(2,1)}, bf16[2,10,128,128]{3,2,1,0:T(8,128)(2,1)S(1)}, u32[]{:S(2)}, u32[]{:S(2)}) %collective-permute-start.15) | collective-permute-done | bytes 655392 | tf_op jit(solution)/shard_map/ppermute | solution.py:26
  70.8 4.3 %collective-permute-done.40.w1 = bf16[384,1280]{1,0:T(8,128)(2,1)S(1)} collective-permute-done((bf16[384,1280]{1,0:T(8,128)(2,1)S(1)}, bf16[384,1280]{1,0:T(8,128)(2,1)S(1)}, u32[]{:S(2)}, u32[]{:S(2)}) %collective-permute-start.40) | collective-permute-done | bytes 983072 | tf_op jit(solution)/shard_map/ppermute | solution.py:26
  75.1 2.7 %collective-permute-start.20 = (bf16[10,128,128]{2,1,0:T(8,128)(2,1)S(1)}, bf16[10,128,128]{2,1,0:T(8,128)(2,1)}, u32[]{:S(2)}, u32[]{:S(2)}) collective-permute-start(bf16[10,128,128]{2,1,0:T(8,128)(2,1)S(1)} %slice_bitcast_fusion), channel_id=1, source_target_pairs={{0,112},{16,0},{32,16},{48,32},{64,48},{80,64},{96,80},{112,96},{1... | collective-permute-start | bytes 983048 | tf_op jit(solution)/shard_map/ppermute | solution.py:26
  80.1 9.1 %shard_map.91 = (f32[8,640,128]{2,1,0:T(8,128)}, f32[2,8,8,128]{3,2,1,0:T(8,128)}) custom-call(s32[8,32]{1,0:T(8,128)} %convert_element_type.3.mask_ref, bf16[256,640]{1,0:T(8,128)(2,1)} %refs_2_.7, bf16[256,640]{1,0:T(8,128)(2,1)} %copy-done.29, bf16[256,640]{1,0:T(8,128)(2,1)} %collective-permute-done.4.refs_2_.refs_4_, ...), custom_call_target="tpu_custom_call" | custom-call | flops 3000000000 | bytes 6291456 | tf_op jit(solution)/shard_map/pallas_call | solution.py:242
  91.6 8.5 %shard_map.92 = (f32[8,640,128]{2,1,0:T(8,128)}, f32[2,8,8,128]{3,2,1,0:T(8,128)}) custom-call(s32[8,32]{1,0:T(8,128)} %convert_element_type.3.mask_ref, f32[8,640,128]{2,1,0:T(8,128)} %get-tuple-element.19.refs_0_, f32[2,8,8,128]{3,2,1,0:T(8,128)} %get-tuple-element.20.refs_1_, bf16[256,640]{1,0:T(8,128)(2,1)} %refs_2_.7, bf16[256,640]{1,0:T(8,128)(2,1)} %copy-done.29, ...), custom_call_target="tpu_custom_call" | custom-call | flops 3000000000 | bytes 4194304 | tf_op jit(solution)/shard_map/pallas_call | solution.py:242
  101.7 8.4 %shard_map.93 = (f32[8,640,128]{2,1,0:T(8,128)}, f32[2,8,8,128]{3,2,1,0:T(8,128)}) custom-call(s32[8,32]{1,0:T(8,128)} %convert_element_type.3.mask_ref, f32[8,640,128]{2,1,0:T(8,128)} %get-tuple-element.21.refs_0_, f32[2,8,8,128]{3,2,1,0:T(8,128)} %get-tuple-element.22.refs_1_, bf16[256,640]{1,0:T(8,128)(2,1)} %refs_2_.7, bf16[256,640]{1,0:T(8,128)(2,1)} %copy-done.29, ...), custom_call_target="tpu_custom_call" | custom-call | flops 3000000000 | bytes 4194304 | tf_op jit(solution)/shard_map/pallas_call | solution.py:242
  111.1 4.6 %shard_map.96 = (bf16[2,416,128]{2,1,0:T(8,128)(2,1)}, bf16[2,416,128]{2,1,0:T(8,128)(2,1)}, bf16[2,416,128]{2,1,0:T(8,128)(2,1)}, bf16[2,416,128]{2,1,0:T(8,128)(2,1)}) custom-call(s32[8,32]{1,0:T(8,128)} %convert_element_type.3.mask_ref, f32[8,640,128]{2,1,0:T(8,128)} %get-tuple-element.23.refs_0_, f32[2,8,8,128]{3,2,1,0:T(8,128)} %get-tuple-element.24.refs_1_, ...), custom_call_target="tpu_custom_call" | custom-call | flops 3000000000 | bytes 2097152 | tf_op jit(solution)/shard_map/pallas_call | solution.py:242
  116.9 4.2 %shard_map.94 = (bf16[2,288,128]{2,1,0:T(8,128)(2,1)}, bf16[2,288,128]{2,1,0:T(8,128)(2,1)}, bf16[2,288,128]{2,1,0:T(8,128)(2,1)}, bf16[2,288,128]{2,1,0:T(8,128)(2,1)}) custom-call(s32[8,32]{1,0:T(8,128)} %convert_element_type.3.mask_ref, f32[8,640,128]{2,1,0:T(8,128)} %get-tuple-element.23.refs_0_, f32[2,8,8,128]{3,2,1,0:T(8,128)} %get-tuple-element.24.refs_1_, ...), custom_call_target="tpu_custom_call" | custom-call | flops 3000000000 | bytes 2097152 | tf_op jit(solution)/shard_map/pallas_call | solution.py:242
  121.1 5.3 %collective-permute-done.31.w3 = bf16[256,1280]{1,0:T(8,128)(2,1)S(1)} collective-permute-done((bf16[256,1280]{1,0:T(8,128)(2,1)S(1)}, bf16[256,1280]{1,0:T(8,128)(2,1)S(1)}, u32[]{:S(2)}, u32[]{:S(2)}) %collective-permute-start.31) | collective-permute-done | bytes 655392 | tf_op jit(solution)/shard_map/ppermute | solution.py:26
  128.2 2.4 %collective-permute-done.23.one = bf16[2,288,128]{2,1,0:T(8,128)(2,1)S(1)} collective-permute-done((bf16[2,288,128]{2,1,0:T(8,128)(2,1)}, bf16[2,288,128]{2,1,0:T(8,128)(2,1)S(1)}, u32[]{:S(2)}, u32[]{:S(2)}) %collective-permute-start.23) | collective-permute-done | bytes 147488 | tf_op jit(solution)/shard_map/ppermute | solution.py:31
  130.6 2.3 %collective-permute-start.24 = (bf16[2,288,128]{2,1,0:T(8,128)(2,1)}, bf16[2,288,128]{2,1,0:T(8,128)(2,1)}, u32[]{:S(2)}, u32[]{:S(2)}) collective-permute-start(bf16[2,288,128]{2,1,0:T(8,128)(2,1)} %get-tuple-element.27), channel_id=1, source_target_pairs={{0,2},{128,130},{2,0},{130,128},{1,3},{129,131},{3,1},{131,129},{4... | collective-permute-start | bytes 442376 | tf_op jit(solution)/shard_map/ppermute | solution.py:31
  133.7 2.6 %collective-permute-start.32 = (bf16[256,1280]{1,0:T(8,128)(2,1)S(1)}, bf16[256,1280]{1,0:T(8,128)(2,1)}, u32[]{:S(2)}, u32[]{:S(2)}) collective-permute-start(bf16[256,1280]{1,0:T(8,128)(2,1)S(1)} %collective-permute-done.31.w3), channel_id=1, source_target_pairs={{0,12},{4,0},{8,4},{12,8},{1,13},{5,1},{9,5},{13,9},{2,14},{6,2},{... | collective-permute-start | bytes 1966088 | tf_op jit(solution)/shard_map/ppermute | solution.py:26
  137.0 2.2 %shard_map.97 = bf16[256,384]{1,0:T(8,128)(2,1)} custom-call(bf16[2,416,128]{2,1,0:T(8,128)(2,1)} %get-tuple-element.29.own, bf16[2,416,128]{2,1,0:T(8,128)(2,1)} %copy-done.6, bf16[2,416,128]{2,1,0:T(8,128)(2,1)} %copy-done.7, bf16[2,416,128]{2,1,0:T(8,128)(2,1)} %copy-done.8), custom_call_target="tpu_custom_call" | custom-call | tf_op jit(solution)/shard_map/pallas_call | solution.py:278
  139.2 2.9 %collective-permute-start.36 = (bf16[256,384]{1,0:T(8,128)(2,1)}, bf16[256,384]{1,0:T(8,128)(2,1)S(1)}, u32[]{:S(2)}, u32[]{:S(2)}) collective-permute-start(bf16[256,384]{1,0:T(8,128)(2,1)} %shard_map.97), channel_id=1, source_target_pairs={{0,0},{1,4},{2,8},{3,12},{4,1},{5,5},{6,9},{7,13},{8,2},{9,6},{10,... | collective-permute-start | bytes 589832 | tf_op jit(solution)/shard_map/ppermute | solution.py:371
  142.2 2.7 %collective-permute-start.37 = (bf16[256,384]{1,0:T(8,128)(2,1)}, bf16[256,384]{1,0:T(8,128)(2,1)S(1)}, u32[]{:S(2)}, u32[]{:S(2)}) collective-permute-start(bf16[256,384]{1,0:T(8,128)(2,1)} %shard_map.97), channel_id=1, source_target_pairs={{0,2},{1,6},{2,10},{3,14},{4,3},{5,7},{6,11},{7,15},{8,0},{9,4},{1... | collective-permute-start | bytes 589832 | tf_op jit(solution)/shard_map/ppermute | solution.py:372
  146.8 6.0 %collective-permute-start.26 = (bf16[256,256]{1,0:T(8,128)(2,1)}, bf16[256,256]{1,0:T(8,128)(2,1)S(1)}, u32[]{:S(2)}, u32[]{:S(2)}) collective-permute-start(bf16[256,256]{1,0:T(8,128)(2,1)} %shard_map.95), channel_id=1, source_target_pairs={{0,0},{1,4},{2,8},{3,12},{4,1},{5,5},{6,9},{7,13},{8,2},{9,6},{10,... | collective-permute-start | bytes 393224 | tf_op jit(solution)/shard_map/ppermute | solution.py:371
  152.9 3.1 %collective-permute-done.36.a = bf16[256,384]{1,0:T(8,128)(2,1)S(1)} collective-permute-done((bf16[256,384]{1,0:T(8,128)(2,1)}, bf16[256,384]{1,0:T(8,128)(2,1)S(1)}, u32[]{:S(2)}, u32[]{:S(2)}) %collective-permute-start.36) | collective-permute-done | bytes 196640 | tf_op jit(solution)/shard_map/ppermute | solution.py:371
  157.2 3.4 %collective-permute-start.27 = (bf16[256,256]{1,0:T(8,128)(2,1)}, bf16[256,256]{1,0:T(8,128)(2,1)S(1)}, u32[]{:S(2)}, u32[]{:S(2)}) collective-permute-start(bf16[256,256]{1,0:T(8,128)(2,1)} %shard_map.95), channel_id=1, source_target_pairs={{0,2},{1,6},{2,10},{3,14},{4,3},{5,7},{6,11},{7,15},{8,0},{9,4},{1... | collective-permute-start | bytes 393224 | tf_op jit(solution)/shard_map/ppermute | solution.py:372
  163.0 4.2 %collective-permute-start.28 = (bf16[256,256]{1,0:T(8,128)(2,1)S(1)}, bf16[256,256]{1,0:T(8,128)(2,1)S(1)}, u32[]{:S(2)}, u32[]{:S(2)}) collective-permute-start(bf16[256,256]{1,0:T(8,128)(2,1)S(1)} %collective-permute-done.26.a), channel_id=1, source_target_pairs={{0,1},{1,0},{2,3},{3,2},{4,5},{5,4},{6,7},{7,6},{8,9},{9,8},{10,11... | collective-permute-start | bytes 393224 | tf_op jit(solution)/shard_map/ppermute | solution.py:35
  169.2 5.1 %project_first.1.refs_1_ = f32[256,1280]{1,0:T(8,128)} custom-call(s32[4]{0:T(128)} %and_select_fusion.1.place_ref, bf16[256,384]{1,0:T(8,128)(2,1)} %copy-done.9, bf16[256,384]{1,0:T(8,128)(2,1)} %copy-done.10, bf16[256,384]{1,0:T(8,128)(2,1)} %copy-done.11, bf16[256,384]{1,0:T(8,128)(2,1)} %copy-done.12, bf16[384,1280]{1,0:T(8,128)(2,1)} %copy-done, ...), custom_call_target="tpu_custom_call" | custom-call | tf_op jit(solution)/shard_map/project_first/pallas_call | solution.py:301
  175.9 4.0 %project.1 = bf16[256,1280]{1,0:T(8,128)(2,1)} custom-call(s32[4]{0:T(128)} %and_select_fusion.1.place_ref, bf16[256,256]{1,0:T(8,128)(2,1)} %copy-done.15, bf16[256,256]{1,0:T(8,128)(2,1)} %copy-done.16, bf16[256,256]{1,0:T(8,128)(2,1)} %copy-done.17, bf16[256,256]{1,0:T(8,128)(2,1)} %copy-done.18, bf16[256,1280]{1,0:T(8,128)(2,1)} %copy-done.1, ...), custom_call_target="tpu_custom_call" | custom-call | tf_op jit(solution)/shard_map/project/pallas_call | solution.py:301
  (150 shorter events, 36.4 us)
Async XLA Ops:
  2.1 21.0 %collective-permute-start.7 = (bf16[2,10,128,128]{3,2,1,0:T(8,128)(2,1)}, bf16[2,10,128,128]{3,2,1,0:T(8,128)(2,1)S(1)}, u32[]{:S(2)}, u32[]{:S(2)}) collective-permute-start(bf16[2,10,128,128]{3,2,1,0:T(8,128)(2,1)} %prepare.1.refs_4_), channel_id=1, source_target_pairs={{0,16},{16,32},{32,48},{48,64},{64,80},{80,96},{96,112},{112,0},{1... | collective-permute-start | bytes 1966088 | tf_op jit(solution)/shard_map/ppermute | solution.py:26
  4.6 18.6 %collective-permute-start.9 = (bf16[2,10,128,128]{3,2,1,0:T(8,128)(2,1)}, bf16[2,10,128,128]{3,2,1,0:T(8,128)(2,1)}, u32[]{:S(2)}, u32[]{:S(2)}) collective-permute-start(bf16[2,10,128,128]{3,2,1,0:T(8,128)(2,1)} %prepare.1.refs_4_), channel_id=1, source_target_pairs={{0,112},{16,0},{32,16},{48,32},{64,48},{80,64},{96,80},{112,96},{1... | collective-permute-start | bytes 1966088 | tf_op jit(solution)/shard_map/ppermute | solution.py:26
  23.1 27.2 %collective-permute-start.11 = (bf16[2,10,128,128]{3,2,1,0:T(8,128)(2,1)S(1)}, bf16[2,10,128,128]{3,2,1,0:T(8,128)(2,1)}, u32[]{:S(2)}, u32[]{:S(2)}) collective-permute-start(bf16[2,10,128,128]{3,2,1,0:T(8,128)(2,1)S(1)} %collective-permute-done.7.refs_6_), channel_id=1, source_target_pairs={{0,16},{16,32},{32,48},{48,64},{64,80},{80,96},{96,112},{112,0},{1... | collective-permute-start | bytes 1966088 | tf_op jit(solution)/shard_map/ppermute | solution.py:26
  23.2 28.7 %collective-permute-start.13 = (bf16[2,10,128,128]{3,2,1,0:T(8,128)(2,1)}, bf16[2,10,128,128]{3,2,1,0:T(8,128)(2,1)}, u32[]{:S(2)}, u32[]{:S(2)}) collective-permute-start(bf16[2,10,128,128]{3,2,1,0:T(8,128)(2,1)} %collective-permute-done.9.refs_8_), channel_id=1, source_target_pairs={{0,112},{16,0},{32,16},{48,32},{64,48},{80,64},{96,80},{112,96},{1... | collective-permute-start | bytes 1966088 | tf_op jit(solution)/shard_map/ppermute | solution.py:26
  25.8 24.5 %collective-permute-start.3 = (bf16[256,640]{1,0:T(8,128)(2,1)}, bf16[256,640]{1,0:T(8,128)(2,1)S(1)}, u32[]{:S(2)}, u32[]{:S(2)}) collective-permute-start(bf16[256,640]{1,0:T(8,128)(2,1)} %refs_2_.7), channel_id=1, source_target_pairs={{0,128},{128,2},{2,130},{130,0},{1,129},{129,3},{3,131},{131,1},{4... | collective-permute-start | bytes 983048 | tf_op jit(solution)/shard_map/ppermute | solution.py:31
  27.0 23.4 %collective-permute-start.4 = (bf16[256,640]{1,0:T(8,128)(2,1)}, bf16[256,640]{1,0:T(8,128)(2,1)}, u32[]{:S(2)}, u32[]{:S(2)}) collective-permute-start(bf16[256,640]{1,0:T(8,128)(2,1)} %refs_2_.7), channel_id=1, source_target_pairs={{0,2},{128,130},{2,0},{130,128},{1,3},{129,131},{3,1},{131,129},{4... | collective-permute-start | bytes 983048 | tf_op jit(solution)/shard_map/ppermute | solution.py:31
  46.5 14.4 %collective-permute-start.6 = (bf16[2,10,128,128]{3,2,1,0:T(8,128)(2,1)}, bf16[2,10,128,128]{3,2,1,0:T(8,128)(2,1)}, u32[]{:S(2)}, u32[]{:S(2)}) collective-permute-start(bf16[2,10,128,128]{3,2,1,0:T(8,128)(2,1)} %prepare.1.refs_4_), channel_id=1, source_target_pairs={{0,1},{1,0},{2,3},{3,2},{4,5},{5,4},{6,7},{7,6},{8,9},{9,8},{10,11... | collective-permute-start | bytes 1966088 | tf_op jit(solution)/shard_map/ppermute | solution.py:35
  50.3 17.6 %collective-permute-start.15 = (bf16[2,10,128,128]{3,2,1,0:T(8,128)(2,1)}, bf16[2,10,128,128]{3,2,1,0:T(8,128)(2,1)S(1)}, u32[]{:S(2)}, u32[]{:S(2)}) collective-permute-start(bf16[2,10,128,128]{3,2,1,0:T(8,128)(2,1)} %collective-permute-done.11.refs_6_), channel_id=1, source_target_pairs={{0,16},{16,32},{32,48},{48,64},{64,80},{80,96},{96,112},{112,0},{1... | collective-permute-start | bytes 1966088 | tf_op jit(solution)/shard_map/ppermute | solution.py:26
  50.5 24.6 %collective-permute-start.40 = (bf16[384,1280]{1,0:T(8,128)(2,1)S(1)}, bf16[384,1280]{1,0:T(8,128)(2,1)S(1)}, u32[]{:S(2)}, u32[]{:S(2)}) collective-permute-start(bf16[384,1280]{1,0:T(8,128)(2,1)S(1)} %slice.26.w0), channel_id=1, source_target_pairs={{0,4},{4,8},{8,12},{12,0},{1,5},{5,9},{9,13},{13,1},{2,6},{6,10},{... | collective-permute-start | bytes 2949128 | tf_op jit(solution)/shard_map/ppermute | solution.py:26
  51.8 17.1 %collective-permute-start.17 = (bf16[2,10,128,128]{3,2,1,0:T(8,128)(2,1)}, bf16[2,10,128,128]{3,2,1,0:T(8,128)(2,1)}, u32[]{:S(2)}, u32[]{:S(2)}) collective-permute-start(bf16[2,10,128,128]{3,2,1,0:T(8,128)(2,1)} %collective-permute-done.13.refs_8_), channel_id=1, source_target_pairs={{0,112},{16,0},{32,16},{48,32},{64,48},{80,64},{96,80},{112,96},{1... | collective-permute-start | bytes 1966088 | tf_op jit(solution)/shard_map/ppermute | solution.py:26
  59.9 15.2 %collective-permute-start.8 = (bf16[2,10,128,128]{3,2,1,0:T(8,128)(2,1)}, bf16[2,10,128,128]{3,2,1,0:T(8,128)(2,1)S(1)}, u32[]{:S(2)}, u32[]{:S(2)}) collective-permute-start(bf16[2,10,128,128]{3,2,1,0:T(8,128)(2,1)} %copy-done.23), channel_id=1, source_target_pairs={{0,1},{1,0},{2,3},{3,2},{4,5},{5,4},{6,7},{7,6},{8,9},{9,8},{10,11... | collective-permute-start | bytes 1966088 | tf_op jit(solution)/shard_map/ppermute | solution.py:35
  60.9 16.9 %collective-permute-start.10 = (bf16[2,10,128,128]{3,2,1,0:T(8,128)(2,1)}, bf16[2,10,128,128]{3,2,1,0:T(8,128)(2,1)}, u32[]{:S(2)}, u32[]{:S(2)}) collective-permute-start(bf16[2,10,128,128]{3,2,1,0:T(8,128)(2,1)} %collective-permute-done.9.refs_8_), channel_id=1, source_target_pairs={{0,1},{1,0},{2,3},{3,2},{4,5},{5,4},{6,7},{7,6},{8,9},{9,8},{10,11... | collective-permute-start | bytes 1966088 | tf_op jit(solution)/shard_map/ppermute | solution.py:35
  67.9 11.3 %collective-permute-start.12 = (bf16[2,10,128,128]{3,2,1,0:T(8,128)(2,1)}, bf16[2,10,128,128]{3,2,1,0:T(8,128)(2,1)S(1)}, u32[]{:S(2)}, u32[]{:S(2)}) collective-permute-start(bf16[2,10,128,128]{3,2,1,0:T(8,128)(2,1)} %collective-permute-done.11.refs_6_), channel_id=1, source_target_pairs={{0,1},{1,0},{2,3},{3,2},{4,5},{5,4},{6,7},{7,6},{8,9},{9,8},{10,11... | collective-permute-start | bytes 1966088 | tf_op jit(solution)/shard_map/ppermute | solution.py:35
  69.0 20.3 %collective-permute-start.14 = (bf16[2,10,128,128]{3,2,1,0:T(8,128)(2,1)}, bf16[2,10,128,128]{3,2,1,0:T(8,128)(2,1)S(1)}, u32[]{:S(2)}, u32[]{:S(2)}) collective-permute-start(bf16[2,10,128,128]{3,2,1,0:T(8,128)(2,1)} %collective-permute-done.13.refs_8_), channel_id=1, source_target_pairs={{0,1},{1,0},{2,3},{3,2},{4,5},{5,4},{6,7},{7,6},{8,9},{9,8},{10,11... | collective-permute-start | bytes 1966088 | tf_op jit(solution)/shard_map/ppermute | solution.py:35
  75.1 15.7 %collective-permute-start.19 = (bf16[10,128,128]{2,1,0:T(8,128)(2,1)S(1)}, bf16[10,128,128]{2,1,0:T(8,128)(2,1)S(1)}, u32[]{:S(2)}, u32[]{:S(2)}) collective-permute-start(bf16[10,128,128]{2,1,0:T(8,128)(2,1)S(1)} %slice_bitcast_fusion.1), channel_id=1, source_target_pairs={{0,16},{16,32},{32,48},{48,64},{64,80},{80,96},{96,112},{112,0},{1... | collective-permute-start | bytes 983048 | tf_op jit(solution)/shard_map/ppermute | solution.py:26
  75.1 16.4 %collective-permute-start.20 = (bf16[10,128,128]{2,1,0:T(8,128)(2,1)S(1)}, bf16[10,128,128]{2,1,0:T(8,128)(2,1)}, u32[]{:S(2)}, u32[]{:S(2)}) collective-permute-start(bf16[10,128,128]{2,1,0:T(8,128)(2,1)S(1)} %slice_bitcast_fusion), channel_id=1, source_target_pairs={{0,112},{16,0},{32,16},{48,32},{64,48},{80,64},{96,80},{112,96},{1... | collective-permute-start | bytes 983048 | tf_op jit(solution)/shard_map/ppermute | solution.py:26
  77.8 22.3 %collective-permute-start.16 = (bf16[2,10,128,128]{3,2,1,0:T(8,128)(2,1)S(1)}, bf16[2,10,128,128]{3,2,1,0:T(8,128)(2,1)S(1)}, u32[]{:S(2)}, u32[]{:S(2)}) collective-permute-start(bf16[2,10,128,128]{3,2,1,0:T(8,128)(2,1)S(1)} %collective-permute-done.15.refs_6_), channel_id=1, source_target_pairs={{0,1},{1,0},{2,3},{3,2},{4,5},{5,4},{6,7},{7,6},{8,9},{9,8},{10,11... | collective-permute-start | bytes 1966088 | tf_op jit(solution)/shard_map/ppermute | solution.py:35
  79.2 21.4 %collective-permute-start.18 = (bf16[2,10,128,128]{3,2,1,0:T(8,128)(2,1)}, bf16[2,10,128,128]{3,2,1,0:T(8,128)(2,1)S(1)}, u32[]{:S(2)}, u32[]{:S(2)}) collective-permute-start(bf16[2,10,128,128]{3,2,1,0:T(8,128)(2,1)} %collective-permute-done.17.refs_8_), channel_id=1, source_target_pairs={{0,1},{1,0},{2,3},{3,2},{4,5},{5,4},{6,7},{7,6},{8,9},{9,8},{10,11... | collective-permute-start | bytes 1966088 | tf_op jit(solution)/shard_map/ppermute | solution.py:35
  89.3 37.1 %collective-permute-start.42 = (bf16[384,1280]{1,0:T(8,128)(2,1)S(1)}, bf16[384,1280]{1,0:T(8,128)(2,1)S(1)}, u32[]{:S(2)}, u32[]{:S(2)}) collective-permute-start(bf16[384,1280]{1,0:T(8,128)(2,1)S(1)} %slice.26.w0), channel_id=1, source_target_pairs={{0,12},{4,0},{8,4},{12,8},{1,13},{5,1},{9,5},{13,9},{2,14},{6,2},{... | collective-permute-start | bytes 2949128 | tf_op jit(solution)/shard_map/ppermute | solution.py:26
  90.9 19.3 %collective-permute-start.21 = (bf16[10,128,128]{2,1,0:T(8,128)(2,1)S(1)}, bf16[10,128,128]{2,1,0:T(8,128)(2,1)S(1)}, u32[]{:S(2)}, u32[]{:S(2)}) collective-permute-start(bf16[10,128,128]{2,1,0:T(8,128)(2,1)S(1)} %collective-permute-done.19.refs_6_), channel_id=1, source_target_pairs={{0,1},{1,0},{2,3},{3,2},{4,5},{5,4},{6,7},{7,6},{8,9},{9,8},{10,11... | collective-permute-start | bytes 983048 | tf_op jit(solution)/shard_map/ppermute | solution.py:35
  91.5 18.7 %collective-permute-start.22 = (bf16[10,128,128]{2,1,0:T(8,128)(2,1)}, bf16[10,128,128]{2,1,0:T(8,128)(2,1)S(1)}, u32[]{:S(2)}, u32[]{:S(2)}) collective-permute-start(bf16[10,128,128]{2,1,0:T(8,128)(2,1)} %collective-permute-done.20.refs_7_), channel_id=1, source_target_pairs={{0,1},{1,0},{2,3},{3,2},{4,5},{5,4},{6,7},{7,6},{8,9},{9,8},{10,11... | collective-permute-start | bytes 983048 | tf_op jit(solution)/shard_map/ppermute | solution.py:35
  100.1 26.3 %collective-permute-start.31 = (bf16[256,1280]{1,0:T(8,128)(2,1)S(1)}, bf16[256,1280]{1,0:T(8,128)(2,1)S(1)}, u32[]{:S(2)}, u32[]{:S(2)}) collective-permute-start(bf16[256,1280]{1,0:T(8,128)(2,1)S(1)} %slice.25.w0), channel_id=1, source_target_pairs={{0,12},{4,0},{8,4},{12,8},{1,13},{5,1},{9,5},{13,9},{2,14},{6,2},{... | collective-permute-start | bytes 1966088 | tf_op jit(solution)/shard_map/ppermute | solution.py:26
  100.7 46.2 %collective-permute-start.41 = (bf16[384,1280]{1,0:T(8,128)(2,1)S(1)}, bf16[384,1280]{1,0:T(8,128)(2,1)}, u32[]{:S(2)}, u32[]{:S(2)}) collective-permute-start(bf16[384,1280]{1,0:T(8,128)(2,1)S(1)} %collective-permute-done.40.w1), channel_id=1, source_target_pairs={{0,4},{4,8},{8,12},{12,0},{1,5},{5,9},{9,13},{13,1},{2,6},{6,10},{... | collective-permute-start | bytes 2949128 | tf_op jit(solution)/shard_map/ppermute | solution.py:26
  115.6 17.2 %collective-permute-start.33 = (bf16[2,416,128]{2,1,0:T(8,128)(2,1)}, bf16[2,416,128]{2,1,0:T(8,128)(2,1)S(1)}, u32[]{:S(2)}, u32[]{:S(2)}) collective-permute-start(bf16[2,416,128]{2,1,0:T(8,128)(2,1)} %get-tuple-element.30), channel_id=1, source_target_pairs={{0,130},{128,0},{2,128},{130,2},{1,131},{129,1},{3,129},{131,3},{4... | collective-permute-start | bytes 638984 | tf_op jit(solution)/shard_map/ppermute | solution.py:31
  115.7 17.2 %collective-permute-start.34 = (bf16[2,416,128]{2,1,0:T(8,128)(2,1)}, bf16[2,416,128]{2,1,0:T(8,128)(2,1)S(1)}, u32[]{:S(2)}, u32[]{:S(2)}) collective-permute-start(bf16[2,416,128]{2,1,0:T(8,128)(2,1)} %get-tuple-element.31), channel_id=1, source_target_pairs={{0,2},{128,130},{2,0},{130,128},{1,3},{129,131},{3,1},{131,129},{4... | collective-permute-start | bytes 638984 | tf_op jit(solution)/shard_map/ppermute | solution.py:31
  132.9 41.4 %collective-permute-start.30 = (bf16[256,1280]{1,0:T(8,128)(2,1)S(1)}, bf16[256,1280]{1,0:T(8,128)(2,1)S(1)}, u32[]{:S(2)}, u32[]{:S(2)}) collective-permute-start(bf16[256,1280]{1,0:T(8,128)(2,1)S(1)} %slice.25.w0), channel_id=1, source_target_pairs={{0,4},{4,8},{8,12},{12,0},{1,5},{5,9},{9,13},{13,1},{2,6},{6,10},{... | collective-permute-start | bytes 1966088 | tf_op jit(solution)/shard_map/ppermute | solution.py:26
  133.7 40.6 %collective-permute-start.32 = (bf16[256,1280]{1,0:T(8,128)(2,1)S(1)}, bf16[256,1280]{1,0:T(8,128)(2,1)}, u32[]{:S(2)}, u32[]{:S(2)}) collective-permute-start(bf16[256,1280]{1,0:T(8,128)(2,1)S(1)} %collective-permute-done.31.w3), channel_id=1, source_target_pairs={{0,12},{4,0},{8,4},{12,8},{1,13},{5,1},{9,5},{13,9},{2,14},{6,2},{... | collective-permute-start | bytes 1966088 | tf_op jit(solution)/shard_map/ppermute | solution.py:26
  139.2 16.8 %collective-permute-start.36 = (bf16[256,384]{1,0:T(8,128)(2,1)}, bf16[256,384]{1,0:T(8,128)(2,1)S(1)}, u32[]{:S(2)}, u32[]{:S(2)}) collective-permute-start(bf16[256,384]{1,0:T(8,128)(2,1)} %shard_map.97), channel_id=1, source_target_pairs={{0,0},{1,4},{2,8},{3,12},{4,1},{5,5},{6,9},{7,13},{8,2},{9,6},{10,... | collective-permute-start | bytes 589832 | tf_op jit(solution)/shard_map/ppermute | solution.py:371
  142.2 18.4 %collective-permute-start.37 = (bf16[256,384]{1,0:T(8,128)(2,1)}, bf16[256,384]{1,0:T(8,128)(2,1)S(1)}, u32[]{:S(2)}, u32[]{:S(2)}) collective-permute-start(bf16[256,384]{1,0:T(8,128)(2,1)} %shard_map.97), channel_id=1, source_target_pairs={{0,2},{1,6},{2,10},{3,14},{4,3},{5,7},{6,11},{7,15},{8,0},{9,4},{1... | collective-permute-start | bytes 589832 | tf_op jit(solution)/shard_map/ppermute | solution.py:372
  146.8 10.3 %collective-permute-start.26 = (bf16[256,256]{1,0:T(8,128)(2,1)}, bf16[256,256]{1,0:T(8,128)(2,1)S(1)}, u32[]{:S(2)}, u32[]{:S(2)}) collective-permute-start(bf16[256,256]{1,0:T(8,128)(2,1)} %shard_map.95), channel_id=1, source_target_pairs={{0,0},{1,4},{2,8},{3,12},{4,1},{5,5},{6,9},{7,13},{8,2},{9,6},{10,... | collective-permute-start | bytes 393224 | tf_op jit(solution)/shard_map/ppermute | solution.py:371
  156.0 11.2 %collective-permute-start.38 = (bf16[256,384]{1,0:T(8,128)(2,1)S(1)}, bf16[256,384]{1,0:T(8,128)(2,1)S(1)}, u32[]{:S(2)}, u32[]{:S(2)}) collective-permute-start(bf16[256,384]{1,0:T(8,128)(2,1)S(1)} %collective-permute-done.36.a), channel_id=1, source_target_pairs={{0,1},{1,0},{2,3},{3,2},{4,5},{5,4},{6,7},{7,6},{8,9},{9,8},{10,11... | collective-permute-start | bytes 589832 | tf_op jit(solution)/shard_map/ppermute | solution.py:35
  163.0 11.3 %collective-permute-start.28 = (bf16[256,256]{1,0:T(8,128)(2,1)S(1)}, bf16[256,256]{1,0:T(8,128)(2,1)S(1)}, u32[]{:S(2)}, u32[]{:S(2)}) collective-permute-start(bf16[256,256]{1,0:T(8,128)(2,1)S(1)} %collective-permute-done.26.a), channel_id=1, source_target_pairs={{0,1},{1,0},{2,3},{3,2},{4,5},{5,4},{6,7},{7,6},{8,9},{9,8},{10,11... | collective-permute-start | bytes 393224 | tf_op jit(solution)/shard_map/ppermute | solution.py:35
  (45 other events, 654.4 us)

commit v2 on v1

v2 whole, which is shorter than its diff:
```python
import functools
import math

import jax
import jax.numpy as jnp
from jax import lax
from jax.experimental import pallas as pl
from jax.experimental.pallas import tpu as pltpu
from jax.sharding import Mesh, PartitionSpec as P


HD = 128
BLOCK = 128
LIST = 16
HEADS = 5
ROWS = 2 * BLOCK
WIDTH = HEADS * HD
TAIL = 32
EMPTY = -1e30
SCALE2 = math.log2(math.e) / HD**0.5

CALLS = [
    [(0, 0), (0, 1), (-1, 0), (1, 0)],
    [(-1, 1), (1, 1), (-2, 0), (2, 0)],
    [(-2, 1), (2, 1), (-3, 0), (3, 0)],
    [(-3, 1), (3, 1), (4, 0)],
    [(4, 1)],
]
AXES = ("xlo", "z", "y", "xhi", "core")


def shift(value, axes, size, steps):
    return lax.ppermute(value, axes, [(i, (i + steps) % size) for i in range(size)])


def shift_x(value, steps):
    at = [2 * (x % 2) + x // 2 for x in range(4)]
    return lax.ppermute(value, ("xlo", "xhi"), [(at[x], at[(x + steps) % 4]) for x in range(4)])


def swap_core(value):
    return lax.ppermute(value, "core", [(0, 1), (1, 0)])


def prepare_kernel(keys, values, out):
    for b in range(2):
        rows = slice(b * BLOCK, (b + 1) * BLOCK)
        for h in range(HEADS):
            cols = slice(h * HD, (h + 1) * HD)
            out[0, b * HEADS + h] = keys[rows, cols]
            out[1, b * HEADS + h] = values[rows, cols].T


def prepare(keys, values):
    return pl.pallas_call(
        prepare_kernel,
        out_shape=jax.ShapeDtypeStruct((2, 2 * HEADS, BLOCK, HD), jnp.bfloat16),
        name="prepare",
    )(keys, values)


def mark_kernel(source, target):
    target[0] = source[0]


def mark(place):
    smem = pl.BlockSpec(memory_space=pltpu.SMEM)
    return pl.pallas_call(
        mark_kernel, in_specs=[smem], out_specs=smem, out_shape=jax.ShapeDtypeStruct((1,), jnp.int32), name="mark"
    )(place)


def attention(number, split, start, last, place, *refs):
    refs = list(refs)
    masks, refs = refs[:4], refs[4:]
    if start:
        sent, refs = refs[:4], refs[4:]
    else:
        q, refs = refs[2], refs[3:]
    pairs = len(CALLS[number])
    sources, refs = refs[: sum(split)], refs[sum(split) :]
    if last:
        outs, refs = refs[:4], refs[4:]
        acc, ml, part, out_sems, refs = refs[0], refs[1], refs[2], refs[3], refs[4:]
    else:
        acc, ml, refs = refs[0], refs[1], refs[2:]
        if start:
            q, refs = refs[0], refs[1:]
    kv, sems, scores, tops, totals, codes, counts = refs

    copies, rest = [], list(sources)
    for i, pieces in enumerate(split):
        if pieces == 1:
            copies.append((rest.pop(0), kv.at[i]))
        else:
            copies += [(rest.pop(0), kv.at[i, 0]), (rest.pop(0), kv.at[i, 1])]
    if start:
        copies += [(source, q.at[i]) for i, source in enumerate(sent)]
    copies = [pltpu.make_async_copy(*copy, sems.at[i]) for i, copy in enumerate(copies)]
    for copy in copies:
        copy.start()

    me = place[0]
    xlo, z, xhi, core = me >> 7, (me >> 4) & 7, (me >> 1) & 1, me & 1
    ids = []
    for step, other in CALLS[number]:
        quarter = 2 * xhi + (1 - core if other else core)
        ids.append(((xlo * 8 + ((z + step) & 7)) * 4 + quarter) * 2)
    n = jnp.int32(0)
    for i in range(8):
        before = n
        for b in range(2 * pairs):
            codes[n] = jnp.int32(i * 64 + b)
            n = n + masks[i // 2][i % 2, ids[b // 2] + b % 2]
        counts[i] = n - before
    codes[n] = jnp.int32(8 * 64)
    trips = (n + 1) >> 1
    tops[...] = jnp.full(tops.shape, EMPTY, jnp.float32)
    totals[...] = jnp.zeros(totals.shape, jnp.float32)
    if start:
        acc[...] = jnp.zeros(acc.shape, jnp.float32)
        ml[0] = jnp.full(ml.shape[1:], EMPTY, jnp.float32)
        ml[1] = jnp.zeros(ml.shape[1:], jnp.float32)
    for copy in copies:
        copy.wait()

    def first_pass(j, carry):
        for u in range(2):
            i = 2 * j + u
            slot, b = codes[i] >> 6, codes[i] & 63
            at = slot & 7
            pair, tile = b >> 1, (b & 1) * HEADS
            q_rows = pl.ds(pl.multiple_of((at & 1) * BLOCK, BLOCK), BLOCK)
            for h in range(HEADS):
                s = (
                    lax.dot_general(
                        kv[pair, 0, tile + h],
                        q[at >> 1, q_rows, h * HD : (h + 1) * HD],
                        (((1,), (1,)), ((), ())),
                        preferred_element_type=jnp.float32,
                    )
                    * SCALE2
                )
                scores[i, h] = s
                tops[slot, h] = jnp.maximum(tops[slot, h], jnp.max(s.reshape(16, 8, BLOCK), axis=0))
        return carry

    lax.fori_loop(0, trips, first_pass, 0)
    line = lax.broadcasted_iota(jnp.int32, (8, BLOCK), 0)

    def middle(i, carry):
        @pl.when(counts[i] > 0)
        def _():
            old = ml[0, i]
            peak = old
            for h in range(HEADS):
                top = jnp.max(tops[i, h], axis=0, keepdims=True)
                peak = jnp.where(line == h, jnp.maximum(peak, top), peak)
            ml[0, i] = peak
            if not start:
                factor = jnp.exp2(old - peak)
                ml[1, i] = ml[1, i] * factor
                for h in range(HEADS):
                    rows = slice(h * HD, (h + 1) * HD)
                    acc[i, rows, :] = acc[i, rows, :] * factor[h : h + 1]

        return carry

    lax.fori_loop(0, 8, middle, 0)

    def second_pass(j, carry):
        for u in range(2):
            i = 2 * j + u
            slot, b = codes[i] >> 6, codes[i] & 63
            pair, tile = b >> 1, (b & 1) * HEADS
            for h in range(HEADS):
                rows = slice(h * HD, (h + 1) * HD)
                p = jnp.exp2(scores[i, h] - ml[0, slot, h : h + 1, :])
                totals[slot, h] = totals[slot, h] + jnp.sum(p.reshape(16, 8, BLOCK), axis=0)
                acc[slot, rows, :] = acc[slot, rows, :] + jnp.dot(
                    kv[pair, 1, tile + h], p.astype(jnp.bfloat16), preferred_element_type=jnp.float32
                )
        return carry

    lax.fori_loop(0, trips, second_pass, 0)

    def sums(i):
        weight = ml[1, i]
        for h in range(HEADS):
            total = jnp.sum(totals[i, h], axis=0, keepdims=True)
            weight = jnp.where(line == h, weight + total, weight)
        return weight

    if not last:

        def finish(i, carry):
            @pl.when(counts[i] > 0)
            def _():
                ml[1, i] = sums(i)

            return carry

        lax.fori_loop(0, 8, finish, 0)
        return

    leaves = []
    for r in range(4):
        for i in (2 * r, 2 * r + 1):
            weight = sums(i)
            some = weight > 0.0
            weight = jnp.where(some, weight, 1.0)
            lse = jnp.where(some, ml[0, i] + jnp.log2(weight), EMPTY)
            scale = 1.0 / weight
            for h in range(HEADS):
                rows = slice(h * HD, (h + 1) * HD)
                part[i, rows, :] = (acc[i, rows, :] * scale[h : h + 1]).astype(jnp.bfloat16)
            tables = []
            for _ in range(3):
                piece = lse.astype(jnp.bfloat16).astype(jnp.float32)
                tables.append(piece)
                lse = lse - piece
            tables.append(jnp.zeros((8, BLOCK), jnp.float32))
            part[i, WIDTH : WIDTH + TAIL, :] = jnp.concatenate(tables, axis=0).astype(jnp.bfloat16)
        leaves.append(pltpu.make_async_copy(part.at[2 * r : 2 * r + 2], outs[r], out_sems.at[r]))
        leaves[-1].start()
    for leave in leaves:
        leave.wait()


def attend(number, place, masks, state, sources):
    start, last = number == 0, number == len(CALLS) - 1
    split = [len(source) if isinstance(source, tuple) else 1 for source in sources]
    sources = [piece for source in sources for piece in (source if isinstance(source, tuple) else (source,))]
    pairs = len(CALLS[number])
    limit = 16 * pairs + 2
    scratch = [
        pltpu.VMEM((pairs, 2, 2 * HEADS, BLOCK, HD), jnp.bfloat16),
        pltpu.SemaphoreType.DMA((len(sources) + 4,)),
        pltpu.VMEM((limit, HEADS, BLOCK, BLOCK), jnp.float32),
        pltpu.VMEM((9, HEADS, 8, BLOCK), jnp.float32),
        pltpu.VMEM((9, HEADS, 8, BLOCK), jnp.float32),
        pltpu.SMEM((limit,), jnp.int32),
        pltpu.SMEM((8,), jnp.int32),
    ]
    hbm, vmem = pl.BlockSpec(memory_space=pltpu.HBM), pl.BlockSpec(memory_space=pltpu.VMEM)
    smem = pl.BlockSpec(memory_space=pltpu.SMEM)
    sums, statistics = ((9, WIDTH, BLOCK), jnp.float32), ((2, 9, 8, BLOCK), jnp.float32)
    aliases = {}
    if last:
        out_specs = [hbm] * 4
        out_shape = [jax.ShapeDtypeStruct((2, WIDTH + TAIL, BLOCK), jnp.bfloat16)] * 4
        scratch = [
            pltpu.VMEM((8, WIDTH + TAIL, BLOCK), jnp.bfloat16),
            pltpu.SemaphoreType.DMA((4,)),
        ] + scratch
        out_specs = out_specs + [vmem, vmem]
        out_shape = out_shape + [pltpu.VMEM(*sums), pltpu.VMEM(*statistics)]
        aliases = {5: 4, 6: 5}
    else:
        out_specs = [vmem, vmem]
        out_shape = [pltpu.VMEM(*sums), pltpu.VMEM(*statistics)]
        if start:
            out_specs.append(vmem)
            out_shape.append(pltpu.VMEM((4, ROWS, WIDTH), jnp.bfloat16))
        else:
            aliases = {5: 0, 6: 1}
    return pl.pallas_call(
        functools.partial(attention, number, split, start, last),
        in_specs=[smem] * 5 + ([hbm] * 4 if start else [vmem] * 3) + [hbm] * len(sources),
        out_specs=out_specs,
        scratch_shapes=scratch,
        out_shape=out_shape,
        input_output_aliases=aliases,
        cost_estimate=pl.CostEstimate(
            flops=2 * 10**9, transcendentals=pairs * 4 * 5 * BLOCK**2, bytes_accessed=pairs * 2**20
        ),
        compiler_params=pltpu.CompilerParams(vmem_limit_bytes=44 * 2**20),
    )(place, *masks, *state, *sources)


def combine_kernel(own, one, two, three, out):
    parts = (own, one, two, three)
    for b in range(2):
        lses = []
        for part in parts:
            table = part[b, WIDTH : WIDTH + TAIL, :].astype(jnp.float32)
            lses.append(table[0:8] + table[8:16] + table[16:24])
        peak = functools.reduce(jnp.maximum, lses)
        shares = [jnp.exp2(lse - peak) for lse in lses]
        whole = 1.0 / (shares[0] + shares[1] + shares[2] + shares[3])
        shares = [share * whole for share in shares]
        for h in range(HEADS):
            rows = slice(h * HD, (h + 1) * HD)
            value = parts[0][b, rows, :].astype(jnp.float32) * shares[0][h : h + 1]
            for part, share in zip(parts[1:], shares[1:]):
                value = value + part[b, rows, :].astype(jnp.float32) * share[h : h + 1]
            out[b * BLOCK : (b + 1) * BLOCK, rows] = value.T.astype(jnp.bfloat16)


def combine(parts):
    return pl.pallas_call(
        combine_kernel, out_shape=jax.ShapeDtypeStruct((ROWS, WIDTH), jnp.bfloat16), name="combine"
    )(*parts)


def project_kernel(place, a, b, c, d, t0, t1, t2, t3, b0, b1, b2, b3, gate, out, rows):
    me = place[0]
    y, rep = (me >> 2) & 3, me & 3
    for piece, group in ((a, rep), (b, rep ^ 2), (c, rep ^ 1), (d, rep ^ 3)):
        rows[(y - group) & 3] = piece[...]
    dot = functools.partial(jnp.dot, preferred_element_type=jnp.float32)
    for i in range(out.shape[1] // 256):
        cols = slice(i * 256, (i + 1) * 256)
        value = dot(rows[0, :, :CUT], t0[:, cols])
        for j, top in ((1, t1), (2, t2), (3, t3)):
            value = value + dot(rows[j, :, :CUT], top[:, cols])
        for j, bottom in enumerate((b0, b1, b2, b3)):
            value = value + dot(rows[j, :, CUT:], bottom[:, cols])
        out[:, cols] = (gate[:, cols] * value).astype(jnp.bfloat16)


def project(place, pieces, weights, gate):
    cols = weights[0].shape[1]
    vmem = pl.BlockSpec(memory_space=pltpu.VMEM)
    return pl.pallas_call(
        project_kernel,
        in_specs=[pl.BlockSpec(memory_space=pltpu.SMEM)] + [vmem] * 13,
        out_specs=vmem,
        scratch_shapes=[pltpu.VMEM((4, ROWS, WIDTH), jnp.bfloat16)],
        out_shape=jax.ShapeDtypeStruct((ROWS, cols), jnp.bfloat16),
        name="project",
    )(place, *pieces, *weights, gate[None, :])


CUT = 384


def stages(queries, keys, values, block_lists, list_counts, out_weight, gate):
    place = mark(lax.axis_index(AXES).astype(jnp.int32).reshape(1))

    own = prepare(keys, values)
    near = {(0, 0): own}
    near[0, 1] = swap_core(own)
    for sign in (1, -1):
        for d in (1, 2, 3):
            near[-sign * d, 0] = shift(near[-sign * (d - 1), 0], "z", 8, sign)
            near[-sign * d, 1] = swap_core(near[-sign * d, 0])
    far_keys = shift(near[-3, 0][0], "z", 8, 1)
    far_values = shift(near[3, 0][1], "z", 8, -1)
    near[4, 0] = (far_keys, far_values)
    far_keys = swap_core(far_keys)
    far_values = swap_core(far_values)
    near[4, 1] = (far_keys, far_values)

    top, bottom = out_weight[:CUT], out_weight[CUT:]
    t1 = shift(top, "y", 4, 1)
    b3 = shift(bottom, "y", 4, -1)
    b1 = shift(bottom, "y", 4, 1)
    t3 = shift(top, "y", 4, -1)
    t2 = shift(t1, "y", 4, 1)
    b2 = shift(b3, "y", 4, -1)

    used = jnp.arange(LIST)[None, :] < list_counts[:, None]
    listed = (block_lists[:, :, None] == jnp.arange(128)[None, None, :]) & used[:, :, None]
    mask = jnp.any(listed, axis=1).astype(jnp.int32)
    masks, state = [mask], [queries]
    for r in (1, 2, 3):
        masks.append(shift_x(mask, r))
        state.append(shift_x(queries, r))

    all_queries = None
    for number, call in enumerate(CALLS):
        result = attend(number, place, masks, state, [near[key] for key in call])
        if number == 0:
            all_queries = result[2]
        state = [result[0], result[1], all_queries]
    parts = result[:4]

    back = [parts[0]]
    for r in (1, 2, 3):
        back.append(shift_x(parts[r], -r))
    attended = combine(back)

    places = [(i, j) for i in range(4) for j in range(4)]
    here = lax.ppermute(attended, ("y", "xhi", "core"), [(4 * i + j, 4 * j + i) for i, j in places])
    there = lax.ppermute(attended, ("y", "xhi", "core"), [(4 * i + j, 4 * j + (i ^ 2)) for i, j in places])
    pieces = [here, there, swap_core(here)]
    pieces.append(swap_core(there))
    return project(place, pieces, [top, t1, t2, t3, bottom, b1, b2, b3], gate)


def solution(mesh):
    fine = Mesh(mesh.devices.reshape(2, 8, 4, 2, 2), AXES)
    rows, rep = ("xlo", "z", "xhi", "core"), ("xhi", "core")
    placed = (P(rows, "y"), P(rows, "y"), P(rows, "y"), P(rows, None), P(rows), P("y", rep), P(rep))
    return jax.shard_map(stages, mesh=fine, in_specs=placed, out_specs=P(("xlo", "z", "y"), rep), check_vma=False)
```

time: 181 us -> 174 us (0.961)
  Pallas kernels: 50.2 us -> 36.5 us
  waiting for transfers between devices: 53.2 us -> 66.6 us
  starting transfers between devices: 64.7 us -> 53.7 us
  local copies, waits for them, and re-layouts: 9.04 us -> 14.5 us
    ppermute x2 -> x1, waiting for transfers between devices: 4.28 us -> 22.9 us  [stages(): lax.ppermute(attended, ('y', 'xhi', 'core'), [(4 * i + j, 4 * j + i) for...]
    pallas_call x7, Pallas kernels: 39 us -> 27.5 us  [the longest x5 24.6 us: attend(): pl.pallas_call(functools.partial(attention, number, split, start, last),...]
    ppermute x14, waiting for transfers between devices: 31.3 us -> 22.6 us  [shift(): lax.ppermute(value, axes, [(i, (i + steps) % size) for i in range(size)])]
    unnamed x69 -> x44, local copies, waits for them, and re-layouts: 4.13 us -> 9.67 us
    ppermute x2 -> x1, starting transfers between devices: 8.93 us -> 3.56 us  [stages(): lax.ppermute(attended, ('y', 'xhi', 'core'), [(4 * i + j, 4 * j + i) for...]
    ppermute x13 -> x11, starting transfers between devices: 14.7 us -> 10.8 us  [swap_core(): return lax.ppermute(value, 'core', [(0, 1), (1, 0)])]
    ppermute x12 -> x9, waiting for transfers between devices: 16.7 us -> 20 us  [shift_x(): lax.ppermute(value, ('xlo', 'xhi'), [(at[x], at[(x + steps) % 4]) for x i...]
    ppermute x2 -> x1, starting transfers between devices: 6.08 us -> 3.3 us  [stages(): lax.ppermute(attended, ('y', 'xhi', 'core'), [(4 * i + j, 4 * j + (i ^ 2)...]
  transfers between devices with their start and end apart: 43 -> 36, of which waited for: 12 -> 13; matrix products, arithmetic and copies ran while one was open for 4% -> 4% of each run, Pallas kernels for 24% -> 16%
where the time goes in v2:
time: 174 us; the launch traced here: 173 us
  waiting for transfers between devices  66.6 us (38%)
  starting transfers between devices  53.7 us (31%)
  Pallas kernels  36.5 us (21%)
  local copies, waits for them, and re-layouts  14.5 us (8%)
    pallas_call x5, Pallas kernels, attend(): pl.pallas_call(functools.partial(attention, number, split, start, last),...  24.6 us
    ppermute x14, starting transfers between devices, shift(): lax.ppermute(value, axes, [(i, (i + steps) % size) for i in range(size)])  24.4 us
    ppermute x1, waiting for transfers between devices, stages(): lax.ppermute(attended, ('y', 'xhi', 'core'), [(4 * i + j, 4 * j + i) for...  22.9 us
    ppermute x14, waiting for transfers between devices, shift(): lax.ppermute(value, axes, [(i, (i + steps) % size) for i in range(size)])  22.6 us
    ppermute x9, waiting for transfers between devices, shift_x(): lax.ppermute(value, ('xlo', 'xhi'), [(at[x], at[(x + steps) % 4]) for x i...  20 us
    ppermute x9, starting transfers between devices, shift_x(): lax.ppermute(value, ('xlo', 'xhi'), [(at[x], at[(x + steps) % 4]) for x i...  11.6 us
    ppermute x11, starting transfers between devices, swap_core(): return lax.ppermute(value, 'core', [(0, 1), (1, 0)])  10.8 us
    unnamed x44, local copies, waits for them, and re-layouts  9.67 us
  transfers between devices with their start and end apart: 36, of which 13 were waited for; matrix products, arithmetic and copies ran while one was open for 4% of the time, Pallas kernels for 16%

profile of v2, /device:TPU:1, one launch (start us, length us, event | category | flops | bytes accessed | tf_op | source)
XLA Modules:
  0.0 173.2 jit_solution(17828352556521179989)
XLA Ops:
  0.0 2.1 %prepare.1.refs_8_ = bf16[2,10,128,128]{3,2,1,0:T(8,128)(2,1)} custom-call(bf16[256,640]{1,0:T(8,128)(2,1)} %keys.1, bf16[256,640]{1,0:T(8,128)(2,1)} %values.1), custom_call_target="tpu_custom_call" | custom-call | tf_op jit(solution)/shard_map/prepare/pallas_call | solution.py:55
  2.1 2.5 %collective-permute-start.7 = (bf16[2,10,128,128]{3,2,1,0:T(8,128)(2,1)}, bf16[2,10,128,128]{3,2,1,0:T(8,128)(2,1)S(1)}, u32[]{:S(2)}, u32[]{:S(2)}) collective-permute-start(bf16[2,10,128,128]{3,2,1,0:T(8,128)(2,1)} %prepare.1.refs_8_), channel_id=1, source_target_pairs={{0,16},{16,32},{32,48},{48,64},{64,80},{80,96},{96,112},{112,0},{1... | collective-permute-start | bytes 1966088 | tf_op jit(solution)/shard_map/ppermute | solution.py:33
  4.5 3.9 %collective-permute-start.8 = (bf16[2,10,128,128]{3,2,1,0:T(8,128)(2,1)}, bf16[2,10,128,128]{3,2,1,0:T(8,128)(2,1)}, u32[]{:S(2)}, u32[]{:S(2)}) collective-permute-start(bf16[2,10,128,128]{3,2,1,0:T(8,128)(2,1)} %prepare.1.refs_8_), channel_id=1, source_target_pairs={{0,112},{16,0},{32,16},{48,32},{64,48},{80,64},{96,80},{112,96},{1... | collective-permute-start | bytes 1966088 | tf_op jit(solution)/shard_map/ppermute | solution.py:33
  8.5 14.7 %collective-permute-done.7.refs_10_ = bf16[2,10,128,128]{3,2,1,0:T(8,128)(2,1)S(1)} collective-permute-done((bf16[2,10,128,128]{3,2,1,0:T(8,128)(2,1)}, bf16[2,10,128,128]{3,2,1,0:T(8,128)(2,1)S(1)}, u32[]{:S(2)}, u32[]{:S(2)}) %collective-permute-start.7) | collective-permute-done | bytes 655392 | tf_op jit(solution)/shard_map/ppermute | solution.py:33
  25.6 3.0 %collective-permute-start.12 = (bf16[2,10,128,128]{3,2,1,0:T(8,128)(2,1)}, bf16[2,10,128,128]{3,2,1,0:T(8,128)(2,1)}, u32[]{:S(2)}, u32[]{:S(2)}) collective-permute-start(bf16[2,10,128,128]{3,2,1,0:T(8,128)(2,1)} %collective-permute-done.8.refs_11_), channel_id=1, source_target_pairs={{0,112},{16,0},{32,16},{48,32},{64,48},{80,64},{96,80},{112,96},{1... | collective-permute-start | bytes 1966088 | tf_op jit(solution)/shard_map/ppermute | solution.py:33
  31.4 3.7 %collective-permute-done.refs_1_ = s32[2,128]{1,0:T(2,128)S(1)} collective-permute-done((s32[2,128]{1,0:T(2,128)S(1)}, s32[2,128]{1,0:T(2,128)S(1)}, u32[]{:S(2)}, u32[]{:S(2)}) %collective-permute-start) | collective-permute-done | bytes 1056 | tf_op jit(solution)/shard_map/ppermute | solution.py:38
  36.8 2.3 %collective-permute-done.1.refs_2_ = s32[2,128]{1,0:T(2,128)S(1)} collective-permute-done((s32[2,128]{1,0:T(2,128)S(1)}, s32[2,128]{1,0:T(2,128)S(1)}, u32[]{:S(2)}, u32[]{:S(2)}) %collective-permute-start.1) | collective-permute-done | bytes 1056 | tf_op jit(solution)/shard_map/ppermute | solution.py:38
  41.9 1.9 %collective-permute-start.4 = (bf16[256,640]{1,0:T(8,128)(2,1)}, bf16[256,640]{1,0:T(8,128)(2,1)S(1)}, u32[]{:S(2)}, u32[]{:S(2)}) collective-permute-start(bf16[256,640]{1,0:T(8,128)(2,1)} %refs_4_.1), channel_id=1, source_target_pairs={{0,2},{128,130},{2,0},{130,128},{1,3},{129,131},{3,1},{131,129},{4... | collective-permute-start | bytes 983048 | tf_op jit(solution)/shard_map/ppermute | solution.py:38
  45.4 4.6 %collective-permute-done.4.refs_6_ = bf16[256,640]{1,0:T(8,128)(2,1)S(1)} collective-permute-done((bf16[256,640]{1,0:T(8,128)(2,1)}, bf16[256,640]{1,0:T(8,128)(2,1)S(1)}, u32[]{:S(2)}, u32[]{:S(2)}) %collective-permute-start.4) | collective-permute-done | bytes 327712 | tf_op jit(solution)/shard_map/ppermute | solution.py:38
  50.8 3.7 %collective-permute-start.10 = (bf16[2,10,128,128]{3,2,1,0:T(8,128)(2,1)}, bf16[2,10,128,128]{3,2,1,0:T(8,128)(2,1)}, u32[]{:S(2)}, u32[]{:S(2)}) collective-permute-start(bf16[2,10,128,128]{3,2,1,0:T(8,128)(2,1)} %collective-permute-done.8.refs_11_), channel_id=1, source_target_pairs={{0,1},{1,0},{2,3},{3,2},{4,5},{5,4},{6,7},{7,6},{8,9},{9,8},{10,11... | collective-permute-start | bytes 1966088 | tf_op jit(solution)/shard_map/ppermute | solution.py:42
  54.5 3.1 %collective-permute-start.16 = (bf16[2,10,128,128]{3,2,1,0:T(8,128)(2,1)}, bf16[2,10,128,128]{3,2,1,0:T(8,128)(2,1)S(1)}, u32[]{:S(2)}, u32[]{:S(2)}) collective-permute-start(bf16[2,10,128,128]{3,2,1,0:T(8,128)(2,1)} %collective-permute-done.12.refs_10_), channel_id=1, source_target_pairs={{0,112},{16,0},{32,16},{48,32},{64,48},{80,64},{96,80},{112,96},{1... | collective-permute-start | bytes 1966088 | tf_op jit(solution)/shard_map/ppermute | solution.py:33
  59.6 1.7 collective-permute-start.9
  62.2 2.2 %slice.14.t0 = bf16[384,1280]{1,0:T(8,128)(2,1)} slice(bf16[640,1280]{1,0:T(8,128)(2,1)} %param.12), slice={[0:384], [0:1280]} | slice | bytes 1966080 | tf_op jit(solution)/shard_map/slice | solution.py:355
  64.4 2.0 %slice.15.b0 = bf16[256,1280]{1,0:T(8,128)(2,1)} slice(bf16[640,1280]{1,0:T(8,128)(2,1)} %param.12), slice={[384:640], [0:1280]} | slice | bytes 1310720 | tf_op jit(solution)/shard_map/slice | solution.py:355
  67.8 4.1 %collective-permute-done.16.refs_10_ = bf16[2,10,128,128]{3,2,1,0:T(8,128)(2,1)S(1)} collective-permute-done((bf16[2,10,128,128]{3,2,1,0:T(8,128)(2,1)}, bf16[2,10,128,128]{3,2,1,0:T(8,128)(2,1)S(1)}, u32[]{:S(2)}, u32[]{:S(2)}) %collective-permute-start.16) | collective-permute-done | bytes 655392 | tf_op jit(solution)/shard_map/ppermute | solution.py:33
  72.9 3.4 %collective-permute-start.20 = (bf16[10,128,128]{2,1,0:T(8,128)(2,1)S(1)}, bf16[10,128,128]{2,1,0:T(8,128)(2,1)S(1)}, u32[]{:S(2)}, u32[]{:S(2)}) collective-permute-start(bf16[10,128,128]{2,1,0:T(8,128)(2,1)S(1)} %slice_bitcast_fusion), channel_id=1, source_target_pairs={{0,112},{16,0},{32,16},{48,32},{64,48},{80,64},{96,80},{112,96},{1... | collective-permute-start | bytes 983048 | tf_op jit(solution)/shard_map/ppermute | solution.py:33
  81.3 5.8 %shard_map.73 = (f32[9,640,128]{2,1,0:T(8,128)S(1)}, f32[2,9,8,128]{3,2,1,0:T(8,128)S(1)}, bf16[4,256,640]{2,1,0:T(8,128)(2,1)S(1)}) custom-call(s32[1]{0:T(128)} %mark.1.place, s32[2,128]{1,0:T(2,128)S(1)} %convert_element_type.3.refs_0_, s32[2,128]{1,0:T(2,128)S(1)} %collective-permute-done.refs_1_, s32[2,128]{1,0:T(2,128)S(1)} %collective-permute-done.1.refs_2_, ...), custom_call_target="tpu_custom_call" | custom-call | flops 2000000000 | bytes 4194304 | tf_op jit(solution)/shard_map/pallas_call | solution.py:267
  88.5 5.1 %shard_map.74 = (f32[9,640,128]{2,1,0:T(8,128)S(1)}, f32[2,9,8,128]{3,2,1,0:T(8,128)S(1)}) custom-call(s32[1]{0:T(128)} %mark.1.place, s32[2,128]{1,0:T(2,128)S(1)} %convert_element_type.3.refs_0_, s32[2,128]{1,0:T(2,128)S(1)} %collective-permute-done.refs_1_, ...), custom_call_target="tpu_custom_call", output_to_operand_aliasing={{0}: (5, {}), {1}: (6, {})} | custom-call | flops 2000000000 | bytes 4194304 | tf_op jit(solution)/shard_map/pallas_call | solution.py:267
  93.6 1.9 %collective-permute-start.21 = (bf16[10,128,128]{2,1,0:T(8,128)(2,1)S(1)}, bf16[10,128,128]{2,1,0:T(8,128)(2,1)S(1)}, u32[]{:S(2)}, u32[]{:S(2)}) collective-permute-start(bf16[10,128,128]{2,1,0:T(8,128)(2,1)S(1)} %collective-permute-done.19.refs_9_), channel_id=1, source_target_pairs={{0,1},{1,0},{2,3},{3,2},{4,5},{5,4},{6,7},{7,6},{8,9},{9,8},{10,11... | collective-permute-start | bytes 983048 | tf_op jit(solution)/shard_map/ppermute | solution.py:42
  95.6 6.7 %shard_map.75 = (f32[9,640,128]{2,1,0:T(8,128)S(1)}, f32[2,9,8,128]{3,2,1,0:T(8,128)S(1)}) custom-call(s32[1]{0:T(128)} %mark.1.place, s32[2,128]{1,0:T(2,128)S(1)} %convert_element_type.3.refs_0_, s32[2,128]{1,0:T(2,128)S(1)} %collective-permute-done.refs_1_, ...), custom_call_target="tpu_custom_call", output_to_operand_aliasing={{0}: (5, {}), {1}: (6, {})} | custom-call | flops 2000000000 | bytes 4194304 | tf_op jit(solution)/shard_map/pallas_call | solution.py:267
  103.8 4.4 %shard_map.76 = (f32[9,640,128]{2,1,0:T(8,128)S(1)}, f32[2,9,8,128]{3,2,1,0:T(8,128)S(1)}) custom-call(s32[1]{0:T(128)} %mark.1.place, s32[2,128]{1,0:T(2,128)S(1)} %convert_element_type.3.refs_0_, s32[2,128]{1,0:T(2,128)S(1)} %collective-permute-done.refs_1_, ...), custom_call_target="tpu_custom_call", output_to_operand_aliasing={{0}: (5, {}), {1}: (6, {})} | custom-call | flops 2000000000 | bytes 3145728 | tf_op jit(solution)/shard_map/pallas_call | solution.py:267
  108.2 2.6 %shard_map.77 = (bf16[2,672,128]{2,1,0:T(8,128)(2,1)S(1)}, bf16[2,672,128]{2,1,0:T(8,128)(2,1)S(1)}, bf16[2,672,128]{2,1,0:T(8,128)(2,1)S(1)}, bf16[2,672,128]{2...) custom-call(s32[1]{0:T(128)} %mark.1.place, ...), custom_call_target="tpu_custom_call", output_to_operand_aliasing={{4}: (5, {}), {5}: (6, {})} | custom-call | flops 2000000000 | bytes 1048576 | tf_op jit(solution)/shard_map/pallas_call | solution.py:267
  111.6 3.3 %collective-permute-start.24 = (bf16[2,672,128]{2,1,0:T(8,128)(2,1)S(1)}, bf16[2,672,128]{2,1,0:T(8,128)(2,1)S(1)}, u32[]{:S(2)}, u32[]{:S(2)}) collective-permute-start(bf16[2,672,128]{2,1,0:T(8,128)(2,1)S(1)} %get-tuple-element.29), channel_id=1, source_target_pairs={{0,2},{128,130},{2,0},{130,128},{1,3},{129,131},{3,1},{131,129},{4... | collective-permute-start | bytes 1032200 | tf_op jit(solution)/shard_map/ppermute | solution.py:38
  114.9 3.8 %collective-permute-done.34.b3 = bf16[256,1280]{1,0:T(8,128)(2,1)} collective-permute-done((bf16[256,1280]{1,0:T(8,128)(2,1)S(1)}, bf16[256,1280]{1,0:T(8,128)(2,1)}, u32[]{:S(2)}, u32[]{:S(2)}) %collective-permute-start.34) | collective-permute-done | bytes 655392 | tf_op jit(solution)/shard_map/ppermute | solution.py:33
  118.7 2.9 %collective-permute-start.32 = (bf16[384,1280]{1,0:T(8,128)(2,1)}, bf16[384,1280]{1,0:T(8,128)(2,1)S(1)}, u32[]{:S(2)}, u32[]{:S(2)}) collective-permute-start(bf16[384,1280]{1,0:T(8,128)(2,1)} %slice.14.t0), channel_id=1, source_target_pairs={{0,12},{4,0},{8,4},{12,8},{1,13},{5,1},{9,5},{13,9},{2,14},{6,2},{... | collective-permute-start | bytes 2949128 | tf_op jit(solution)/shard_map/ppermute | solution.py:33
  122.7 2.6 %collective-permute-start.35 = (bf16[256,1280]{1,0:T(8,128)(2,1)}, bf16[256,1280]{1,0:T(8,128)(2,1)}, u32[]{:S(2)}, u32[]{:S(2)}) collective-permute-start(bf16[256,1280]{1,0:T(8,128)(2,1)} %collective-permute-done.34.b3), channel_id=1, source_target_pairs={{0,12},{4,0},{8,4},{12,8},{1,13},{5,1},{9,5},{13,9},{2,14},{6,2},{... | collective-permute-start | bytes 1966088 | tf_op jit(solution)/shard_map/ppermute | solution.py:33
  125.3 5.5 %collective-permute-done.25.three = bf16[2,672,128]{2,1,0:T(8,128)(2,1)S(1)} collective-permute-done((bf16[2,672,128]{2,1,0:T(8,128)(2,1)S(1)}, bf16[2,672,128]{2,1,0:T(8,128)(2,1)S(1)}, u32[]{:S(2)}, u32[]{:S(2)}) %collective-permute-start.25) | collective-permute-done | bytes 344096 | tf_op jit(solution)/shard_map/ppermute | solution.py:38
  131.5 2.4 %combine.1 = bf16[256,640]{1,0:T(8,128)(2,1)} custom-call(bf16[2,672,128]{2,1,0:T(8,128)(2,1)} %copy-done.1, bf16[2,672,128]{2,1,0:T(8,128)(2,1)} %copy-done.15, bf16[2,672,128]{2,1,0:T(8,128)(2,1)} %copy-done.16, bf16[2,672,128]{2,1,0:T(8,128)(2,1)} %copy-done.17), custom_call_target="tpu_custom_call" | custom-call | tf_op jit(solution)/shard_map/combine/pallas_call | solution.py:301
  133.9 3.6 %collective-permute-start.26 = (bf16[256,640]{1,0:T(8,128)(2,1)}, bf16[256,640]{1,0:T(8,128)(2,1)S(1)}, u32[]{:S(2)}, u32[]{:S(2)}) collective-permute-start(bf16[256,640]{1,0:T(8,128)(2,1)} %combine.1), channel_id=1, source_target_pairs={{0,0},{1,4},{2,8},{3,12},{4,1},{5,5},{6,9},{7,13},{8,2},{9,6},{10,... | collective-permute-start | bytes 983048 | tf_op jit(solution)/shard_map/ppermute | solution.py:385
  137.5 3.3 %collective-permute-start.27 = (bf16[256,640]{1,0:T(8,128)(2,1)}, bf16[256,640]{1,0:T(8,128)(2,1)S(1)}, u32[]{:S(2)}, u32[]{:S(2)}) collective-permute-start(bf16[256,640]{1,0:T(8,128)(2,1)} %combine.1), channel_id=1, source_target_pairs={{0,2},{1,6},{2,10},{3,14},{4,3},{5,7},{6,11},{7,15},{8,0},{9,4},{1... | collective-permute-start | bytes 983048 | tf_op jit(solution)/shard_map/ppermute | solution.py:386
  140.8 22.9 %collective-permute-done.26.a = bf16[256,640]{1,0:T(8,128)(2,1)S(1)} collective-permute-done((bf16[256,640]{1,0:T(8,128)(2,1)}, bf16[256,640]{1,0:T(8,128)(2,1)S(1)}, u32[]{:S(2)}, u32[]{:S(2)}) %collective-permute-start.26) | collective-permute-done | bytes 327712 | tf_op jit(solution)/shard_map/ppermute | solution.py:385
  166.2 7.0 %project.1 = bf16[256,1280]{1,0:T(8,128)(2,1)} custom-call(s32[1]{0:T(128)} %mark.1.place, bf16[256,640]{1,0:T(8,128)(2,1)} %copy-done.18, bf16[256,640]{1,0:T(8,128)(2,1)} %copy-done.19, bf16[256,640]{1,0:T(8,128)(2,1)} %copy-done.20, bf16[256,640]{1,0:T(8,128)(2,1)} %collective-permute-done.29.d, bf16[384,1280]{1,0:T(8,128)(2,1)} %slice.14.t0, ...), custom_call_target="tpu_custom_call" | custom-call | tf_op jit(solution)/shard_map/project/pallas_call | solution.py:325
  (101 shorter events, 30.3 us)
Async XLA Ops:
  2.1 21.1 %collective-permute-start.7 = (bf16[2,10,128,128]{3,2,1,0:T(8,128)(2,1)}, bf16[2,10,128,128]{3,2,1,0:T(8,128)(2,1)S(1)}, u32[]{:S(2)}, u32[]{:S(2)}) collective-permute-start(bf16[2,10,128,128]{3,2,1,0:T(8,128)(2,1)} %prepare.1.refs_8_), channel_id=1, source_target_pairs={{0,16},{16,32},{32,48},{48,64},{64,80},{80,96},{96,112},{112,0},{1... | collective-permute-start | bytes 1966088 | tf_op jit(solution)/shard_map/ppermute | solution.py:33
  4.5 21.1 %collective-permute-start.8 = (bf16[2,10,128,128]{3,2,1,0:T(8,128)(2,1)}, bf16[2,10,128,128]{3,2,1,0:T(8,128)(2,1)}, u32[]{:S(2)}, u32[]{:S(2)}) collective-permute-start(bf16[2,10,128,128]{3,2,1,0:T(8,128)(2,1)} %prepare.1.refs_8_), channel_id=1, source_target_pairs={{0,112},{16,0},{32,16},{48,32},{64,48},{80,64},{96,80},{112,96},{1... | collective-permute-start | bytes 1966088 | tf_op jit(solution)/shard_map/ppermute | solution.py:33
  23.2 20.7 %collective-permute-start.11 = (bf16[2,10,128,128]{3,2,1,0:T(8,128)(2,1)S(1)}, bf16[2,10,128,128]{3,2,1,0:T(8,128)(2,1)S(1)}, u32[]{:S(2)}, u32[]{:S(2)}) collective-permute-start(bf16[2,10,128,128]{3,2,1,0:T(8,128)(2,1)S(1)} %collective-permute-done.7.refs_10_), channel_id=1, source_target_pairs={{0,16},{16,32},{32,48},{48,64},{64,80},{80,96},{96,112},{112,0},{1... | collective-permute-start | bytes 1966088 | tf_op jit(solution)/shard_map/ppermute | solution.py:33
  23.2 38.1 %collective-permute-start.6 = (bf16[2,10,128,128]{3,2,1,0:T(8,128)(2,1)}, bf16[2,10,128,128]{3,2,1,0:T(8,128)(2,1)S(1)}, u32[]{:S(2)}, u32[]{:S(2)}) collective-permute-start(bf16[2,10,128,128]{3,2,1,0:T(8,128)(2,1)} %prepare.1.refs_8_), channel_id=1, source_target_pairs={{0,1},{1,0},{2,3},{3,2},{4,5},{5,4},{6,7},{7,6},{8,9},{9,8},{10,11... | collective-permute-start | bytes 1966088 | tf_op jit(solution)/shard_map/ppermute | solution.py:42
  24.4 19.4 %collective-permute-start.3 = (bf16[256,640]{1,0:T(8,128)(2,1)}, bf16[256,640]{1,0:T(8,128)(2,1)S(1)}, u32[]{:S(2)}, u32[]{:S(2)}) collective-permute-start(bf16[256,640]{1,0:T(8,128)(2,1)} %refs_4_.1), channel_id=1, source_target_pairs={{0,128},{128,2},{2,130},{130,0},{1,129},{129,3},{3,131},{131,1},{4... | collective-permute-start | bytes 983048 | tf_op jit(solution)/shard_map/ppermute | solution.py:38
  25.6 28.8 %collective-permute-start.12 = (bf16[2,10,128,128]{3,2,1,0:T(8,128)(2,1)}, bf16[2,10,128,128]{3,2,1,0:T(8,128)(2,1)}, u32[]{:S(2)}, u32[]{:S(2)}) collective-permute-start(bf16[2,10,128,128]{3,2,1,0:T(8,128)(2,1)} %collective-permute-done.8.refs_11_), channel_id=1, source_target_pairs={{0,112},{16,0},{32,16},{48,32},{64,48},{80,64},{96,80},{112,96},{1... | collective-permute-start | bytes 1966088 | tf_op jit(solution)/shard_map/ppermute | solution.py:33
  30.1 5.0 %collective-permute-start = (s32[2,128]{1,0:T(2,128)S(1)}, s32[2,128]{1,0:T(2,128)S(1)}, u32[]{:S(2)}, u32[]{:S(2)}) collective-permute-start(s32[2,128]{1,0:T(2,128)S(1)} %convert_element_type.3.refs_0_), channel_id=1, source_target_pairs={{0,128},{128,2},{2,130},{130,0},{1,129},{129,3},{3,131},{131,1},{4... | collective-permute-start | bytes 3080 | tf_op jit(solution)/shard_map/ppermute | solution.py:38
  41.9 8.2 %collective-permute-start.4 = (bf16[256,640]{1,0:T(8,128)(2,1)}, bf16[256,640]{1,0:T(8,128)(2,1)S(1)}, u32[]{:S(2)}, u32[]{:S(2)}) collective-permute-start(bf16[256,640]{1,0:T(8,128)(2,1)} %refs_4_.1), channel_id=1, source_target_pairs={{0,2},{128,130},{2,0},{130,128},{1,3},{129,131},{3,1},{131,129},{4... | collective-permute-start | bytes 983048 | tf_op jit(solution)/shard_map/ppermute | solution.py:38
  43.8 23.1 %collective-permute-start.15 = (bf16[2,10,128,128]{3,2,1,0:T(8,128)(2,1)S(1)}, bf16[2,10,128,128]{3,2,1,0:T(8,128)(2,1)S(1)}, u32[]{:S(2)}, u32[]{:S(2)}) collective-permute-start(bf16[2,10,128,128]{3,2,1,0:T(8,128)(2,1)S(1)} %collective-permute-done.11.refs_9_), channel_id=1, source_target_pairs={{0,16},{16,32},{32,48},{48,64},{64,80},{80,96},{96,112},{112,0},{1... | collective-permute-start | bytes 1966088 | tf_op jit(solution)/shard_map/ppermute | solution.py:33
  44.6 14.3 %collective-permute-start.5 = (bf16[256,640]{1,0:T(8,128)(2,1)}, bf16[256,640]{1,0:T(8,128)(2,1)S(1)}, u32[]{:S(2)}, u32[]{:S(2)}) collective-permute-start(bf16[256,640]{1,0:T(8,128)(2,1)} %refs_4_.1), channel_id=1, source_target_pairs={{0,130},{128,0},{2,128},{130,2},{1,131},{129,1},{3,129},{131,3},{4... | collective-permute-start | bytes 983048 | tf_op jit(solution)/shard_map/ppermute | solution.py:38
  50.8 16.7 %collective-permute-start.10 = (bf16[2,10,128,128]{3,2,1,0:T(8,128)(2,1)}, bf16[2,10,128,128]{3,2,1,0:T(8,128)(2,1)}, u32[]{:S(2)}, u32[]{:S(2)}) collective-permute-start(bf16[2,10,128,128]{3,2,1,0:T(8,128)(2,1)} %collective-permute-done.8.refs_11_), channel_id=1, source_target_pairs={{0,1},{1,0},{2,3},{3,2},{4,5},{5,4},{6,7},{7,6},{8,9},{9,8},{10,11... | collective-permute-start | bytes 1966088 | tf_op jit(solution)/shard_map/ppermute | solution.py:42
  54.5 17.5 %collective-permute-start.16 = (bf16[2,10,128,128]{3,2,1,0:T(8,128)(2,1)}, bf16[2,10,128,128]{3,2,1,0:T(8,128)(2,1)S(1)}, u32[]{:S(2)}, u32[]{:S(2)}) collective-permute-start(bf16[2,10,128,128]{3,2,1,0:T(8,128)(2,1)} %collective-permute-done.12.refs_10_), channel_id=1, source_target_pairs={{0,112},{16,0},{32,16},{48,32},{64,48},{80,64},{96,80},{112,96},{1... | collective-permute-start | bytes 1966088 | tf_op jit(solution)/shard_map/ppermute | solution.py:33
  59.6 13.2 %collective-permute-start.9 = (bf16[2,10,128,128]{3,2,1,0:T(8,128)(2,1)S(1)}, bf16[2,10,128,128]{3,2,1,0:T(8,128)(2,1)}, u32[]{:S(2)}, u32[]{:S(2)}) collective-permute-start(bf16[2,10,128,128]{3,2,1,0:T(8,128)(2,1)S(1)} %collective-permute-done.7.refs_10_), channel_id=1, source_target_pairs={{0,1},{1,0},{2,3},{3,2},{4,5},{5,4},{6,7},{7,6},{8,9},{9,8},{10,11... | collective-permute-start | bytes 1966088 | tf_op jit(solution)/shard_map/ppermute | solution.py:42
  62.2 10.8 %collective-permute-start.13 = (bf16[2,10,128,128]{3,2,1,0:T(8,128)(2,1)S(1)}, bf16[2,10,128,128]{3,2,1,0:T(8,128)(2,1)}, u32[]{:S(2)}, u32[]{:S(2)}) collective-permute-start(bf16[2,10,128,128]{3,2,1,0:T(8,128)(2,1)S(1)} %collective-permute-done.11.refs_9_), channel_id=1, source_target_pairs={{0,1},{1,0},{2,3},{3,2},{4,5},{5,4},{6,7},{7,6},{8,9},{9,8},{10,11... | collective-permute-start | bytes 1966088 | tf_op jit(solution)/shard_map/ppermute | solution.py:42
  66.9 20.2 %collective-permute-start.14 = (bf16[2,10,128,128]{3,2,1,0:T(8,128)(2,1)}, bf16[2,10,128,128]{3,2,1,0:T(8,128)(2,1)S(1)}, u32[]{:S(2)}, u32[]{:S(2)}) collective-permute-start(bf16[2,10,128,128]{3,2,1,0:T(8,128)(2,1)} %collective-permute-done.12.refs_10_), channel_id=1, source_target_pairs={{0,1},{1,0},{2,3},{3,2},{4,5},{5,4},{6,7},{7,6},{8,9},{9,8},{10,11... | collective-permute-start | bytes 1966088 | tf_op jit(solution)/shard_map/ppermute | solution.py:42
  67.6 34.7 %collective-permute-start.17 = (bf16[2,10,128,128]{3,2,1,0:T(8,128)(2,1)S(1)}, bf16[2,10,128,128]{3,2,1,0:T(8,128)(2,1)S(1)}, u32[]{:S(2)}, u32[]{:S(2)}) collective-permute-start(bf16[2,10,128,128]{3,2,1,0:T(8,128)(2,1)S(1)} %collective-permute-done.15.refs_9_), channel_id=1, source_target_pairs={{0,1},{1,0},{2,3},{3,2},{4,5},{5,4},{6,7},{7,6},{8,9},{9,8},{10,11... | collective-permute-start | bytes 1966088 | tf_op jit(solution)/shard_map/ppermute | solution.py:42
  71.9 31.8 %collective-permute-start.18 = (bf16[2,10,128,128]{3,2,1,0:T(8,128)(2,1)S(1)}, bf16[2,10,128,128]{3,2,1,0:T(8,128)(2,1)S(1)}, u32[]{:S(2)}, u32[]{:S(2)}) collective-permute-start(bf16[2,10,128,128]{3,2,1,0:T(8,128)(2,1)S(1)} %collective-permute-done.16.refs_10_), channel_id=1, source_target_pairs={{0,1},{1,0},{2,3},{3,2},{4,5},{5,4},{6,7},{7,6},{8,9},{9,8},{10,11... | collective-permute-start | bytes 1966088 | tf_op jit(solution)/shard_map/ppermute | solution.py:42
  72.8 20.8 %collective-permute-start.19 = (bf16[10,128,128]{2,1,0:T(8,128)(2,1)S(1)}, bf16[10,128,128]{2,1,0:T(8,128)(2,1)S(1)}, u32[]{:S(2)}, u32[]{:S(2)}) collective-permute-start(bf16[10,128,128]{2,1,0:T(8,128)(2,1)S(1)} %slice_bitcast_fusion.1), channel_id=1, source_target_pairs={{0,16},{16,32},{32,48},{48,64},{64,80},{80,96},{96,112},{112,0},{1... | collective-permute-start | bytes 983048 | tf_op jit(solution)/shard_map/ppermute | solution.py:33
  72.9 22.5 %collective-permute-start.20 = (bf16[10,128,128]{2,1,0:T(8,128)(2,1)S(1)}, bf16[10,128,128]{2,1,0:T(8,128)(2,1)S(1)}, u32[]{:S(2)}, u32[]{:S(2)}) collective-permute-start(bf16[10,128,128]{2,1,0:T(8,128)(2,1)S(1)} %slice_bitcast_fusion), channel_id=1, source_target_pairs={{0,112},{16,0},{32,16},{48,32},{64,48},{80,64},{96,80},{112,96},{1... | collective-permute-start | bytes 983048 | tf_op jit(solution)/shard_map/ppermute | solution.py:33
  87.1 31.6 %collective-permute-start.30 = (bf16[384,1280]{1,0:T(8,128)(2,1)}, bf16[384,1280]{1,0:T(8,128)(2,1)S(1)}, u32[]{:S(2)}, u32[]{:S(2)}) collective-permute-start(bf16[384,1280]{1,0:T(8,128)(2,1)} %slice.14.t0), channel_id=1, source_target_pairs={{0,4},{4,8},{8,12},{12,0},{1,5},{5,9},{9,13},{13,1},{2,6},{6,10},{... | collective-permute-start | bytes 2949128 | tf_op jit(solution)/shard_map/ppermute | solution.py:33
  93.6 14.5 %collective-permute-start.21 = (bf16[10,128,128]{2,1,0:T(8,128)(2,1)S(1)}, bf16[10,128,128]{2,1,0:T(8,128)(2,1)S(1)}, u32[]{:S(2)}, u32[]{:S(2)}) collective-permute-start(bf16[10,128,128]{2,1,0:T(8,128)(2,1)S(1)} %collective-permute-done.19.refs_9_), channel_id=1, source_target_pairs={{0,1},{1,0},{2,3},{3,2},{4,5},{5,4},{6,7},{7,6},{8,9},{9,8},{10,11... | collective-permute-start | bytes 983048 | tf_op jit(solution)/shard_map/ppermute | solution.py:42
  95.5 12.7 %collective-permute-start.22 = (bf16[10,128,128]{2,1,0:T(8,128)(2,1)S(1)}, bf16[10,128,128]{2,1,0:T(8,128)(2,1)S(1)}, u32[]{:S(2)}, u32[]{:S(2)}) collective-permute-start(bf16[10,128,128]{2,1,0:T(8,128)(2,1)S(1)} %collective-permute-done.20.refs_10_), channel_id=1, source_target_pairs={{0,1},{1,0},{2,3},{3,2},{4,5},{5,4},{6,7},{7,6},{8,9},{9,8},{10,11... | collective-permute-start | bytes 983048 | tf_op jit(solution)/shard_map/ppermute | solution.py:42
  102.3 16.4 %collective-permute-start.34 = (bf16[256,1280]{1,0:T(8,128)(2,1)S(1)}, bf16[256,1280]{1,0:T(8,128)(2,1)}, u32[]{:S(2)}, u32[]{:S(2)}) collective-permute-start(bf16[256,1280]{1,0:T(8,128)(2,1)S(1)} %copy-done.11), channel_id=1, source_target_pairs={{0,12},{4,0},{8,4},{12,8},{1,13},{5,1},{9,5},{13,9},{2,14},{6,2},{... | collective-permute-start | bytes 1966088 | tf_op jit(solution)/shard_map/ppermute | solution.py:33
  111.5 10.1 %collective-permute-start.23 = (bf16[2,672,128]{2,1,0:T(8,128)(2,1)S(1)}, bf16[2,672,128]{2,1,0:T(8,128)(2,1)S(1)}, u32[]{:S(2)}, u32[]{:S(2)}) collective-permute-start(bf16[2,672,128]{2,1,0:T(8,128)(2,1)S(1)} %get-tuple-element.28), channel_id=1, source_target_pairs={{0,130},{128,0},{2,128},{130,2},{1,131},{129,1},{3,129},{131,3},{4... | collective-permute-start | bytes 1032200 | tf_op jit(solution)/shard_map/ppermute | solution.py:38
  111.5 26.0 %collective-permute-start.33 = (bf16[256,1280]{1,0:T(8,128)(2,1)S(1)}, bf16[256,1280]{1,0:T(8,128)(2,1)S(1)}, u32[]{:S(2)}, u32[]{:S(2)}) collective-permute-start(bf16[256,1280]{1,0:T(8,128)(2,1)S(1)} %copy-done.11), channel_id=1, source_target_pairs={{0,4},{4,8},{8,12},{12,0},{1,5},{5,9},{9,13},{13,1},{2,6},{6,10},{... | collective-permute-start | bytes 1966088 | tf_op jit(solution)/shard_map/ppermute | solution.py:33
  111.6 11.1 %collective-permute-start.24 = (bf16[2,672,128]{2,1,0:T(8,128)(2,1)S(1)}, bf16[2,672,128]{2,1,0:T(8,128)(2,1)S(1)}, u32[]{:S(2)}, u32[]{:S(2)}) collective-permute-start(bf16[2,672,128]{2,1,0:T(8,128)(2,1)S(1)} %get-tuple-element.29), channel_id=1, source_target_pairs={{0,2},{128,130},{2,0},{130,128},{1,3},{129,131},{3,1},{131,129},{4... | collective-permute-start | bytes 1032200 | tf_op jit(solution)/shard_map/ppermute | solution.py:38
  118.7 12.1 %collective-permute-start.25 = (bf16[2,672,128]{2,1,0:T(8,128)(2,1)S(1)}, bf16[2,672,128]{2,1,0:T(8,128)(2,1)S(1)}, u32[]{:S(2)}, u32[]{:S(2)}) collective-permute-start(bf16[2,672,128]{2,1,0:T(8,128)(2,1)S(1)} %get-tuple-element.30), channel_id=1, source_target_pairs={{0,128},{128,2},{2,130},{130,0},{1,129},{129,3},{3,131},{131,1},{4... | collective-permute-start | bytes 1032200 | tf_op jit(solution)/shard_map/ppermute | solution.py:38
  118.7 46.2 %collective-permute-start.32 = (bf16[384,1280]{1,0:T(8,128)(2,1)}, bf16[384,1280]{1,0:T(8,128)(2,1)S(1)}, u32[]{:S(2)}, u32[]{:S(2)}) collective-permute-start(bf16[384,1280]{1,0:T(8,128)(2,1)} %slice.14.t0), channel_id=1, source_target_pairs={{0,12},{4,0},{8,4},{12,8},{1,13},{5,1},{9,5},{13,9},{2,14},{6,2},{... | collective-permute-start | bytes 2949128 | tf_op jit(solution)/shard_map/ppermute | solution.py:33
  121.6 43.3 %collective-permute-start.31 = (bf16[384,1280]{1,0:T(8,128)(2,1)S(1)}, bf16[384,1280]{1,0:T(8,128)(2,1)}, u32[]{:S(2)}, u32[]{:S(2)}) collective-permute-start(bf16[384,1280]{1,0:T(8,128)(2,1)S(1)} %collective-permute-done.30.t1), channel_id=1, source_target_pairs={{0,4},{4,8},{8,12},{12,0},{1,5},{5,9},{9,13},{13,1},{2,6},{6,10},{... | collective-permute-start | bytes 2949128 | tf_op jit(solution)/shard_map/ppermute | solution.py:33
  122.7 42.2 %collective-permute-start.35 = (bf16[256,1280]{1,0:T(8,128)(2,1)}, bf16[256,1280]{1,0:T(8,128)(2,1)}, u32[]{:S(2)}, u32[]{:S(2)}) collective-permute-start(bf16[256,1280]{1,0:T(8,128)(2,1)} %collective-permute-done.34.b3), channel_id=1, source_target_pairs={{0,12},{4,0},{8,4},{12,8},{1,13},{5,1},{9,5},{13,9},{2,14},{6,2},{... | collective-permute-start | bytes 1966088 | tf_op jit(solution)/shard_map/ppermute | solution.py:33
  133.9 29.8 %collective-permute-start.26 = (bf16[256,640]{1,0:T(8,128)(2,1)}, bf16[256,640]{1,0:T(8,128)(2,1)S(1)}, u32[]{:S(2)}, u32[]{:S(2)}) collective-permute-start(bf16[256,640]{1,0:T(8,128)(2,1)} %combine.1), channel_id=1, source_target_pairs={{0,0},{1,4},{2,8},{3,12},{4,1},{5,5},{6,9},{7,13},{8,2},{9,6},{10,... | collective-permute-start | bytes 983048 | tf_op jit(solution)/shard_map/ppermute | solution.py:385
  137.5 26.3 %collective-permute-start.27 = (bf16[256,640]{1,0:T(8,128)(2,1)}, bf16[256,640]{1,0:T(8,128)(2,1)S(1)}, u32[]{:S(2)}, u32[]{:S(2)}) collective-permute-start(bf16[256,640]{1,0:T(8,128)(2,1)} %combine.1), channel_id=1, source_target_pairs={{0,2},{1,6},{2,10},{3,14},{4,3},{5,7},{6,11},{7,15},{8,0},{9,4},{1... | collective-permute-start | bytes 983048 | tf_op jit(solution)/shard_map/ppermute | solution.py:386
  (26 other events, 255.6 us)
